TPU v7x, 256 devices: a whole 4x4x8 slice. The times are simulated.
256 devices in a mesh: inst: 8 (over x, core), axial: 32 (over y, z).
Axes of the slice: x: 4, y: 4, z: 8, core: 2. Of those that a mesh axis runs over, the one named last changes fastest.
Arguments:
- flow_state: float32 [32, 512, 320], P('inst', 'axial'), may hold values from -6 to 6
- forcing: float32 [32, 512, 320], P('inst', 'axial'), may hold values from -6 to 6
- tile_inverse: bfloat16 [512, 320, 320], P('axial')
- coupling: bfloat16 [512, 320, 320], P('axial')
- sweep_order: int32 [512], P('axial'), may hold values from 0 to 15, as said below
Outputs:
- final_state: float32 [32, 512, 320], P('inst', 'axial')
Inputs may be any that keep to these rules, and one draw needn't show every extreme that they name: `sweep_order`: the 16 entries of each axial group form a permutation of 0 to 15.
All inputs are finite; a program needn't handle non-finite values.
Results may differ from a plain program's by a relative error of at most 0.0003.
Values sent between devices are 32-bit elements; how exact they have to be, the bound alone decides.
A program may use at most 128 MiB of HBM per device.

v0:
```python
import jax
import jax.numpy as jnp
from jax import lax
from jax.sharding import PartitionSpec as P

ITERS = 2


highest = lax.Precision.HIGHEST
spectral_gain = 2.0


def passed_along(value, axis, steps):
    count = lax.axis_size(axis)
    leading, last = (max(0, -steps), min(count, count - steps))
    return lax.ppermute(value, axis, [(source, source + steps) for source in range(leading, last)])


def spectral_rows(row_ids, col_ids, period):
    distance = row_ids[:, None] - col_ids[None, :]
    parity = 1.0 - 2.0 * jnp.mod(distance, 2).astype(jnp.float32)
    angles = jnp.pi * distance.astype(jnp.float32) / period
    on_diag = distance == 0
    sine_safe = jnp.where(on_diag, 1.0, jnp.sin(angles))
    return jnp.where(on_diag, 0.0, 0.5 * parity * jnp.cos(angles) / sine_safe)


def visit_tile(upstream, tile_items):
    right_side, inverse, couple_tile = tile_items
    collapsed_result = right_side - jnp.dot(
        upstream, couple_tile.astype(jnp.float32).T, precision=highest
    )
    updated = jnp.dot(collapsed_result, inverse.astype(jnp.float32).T, precision=highest)
    return (updated, updated)


def compose_tile(running, tile_items):
    inverse, couple_tile = tile_items
    linear_part = -jnp.dot(
        couple_tile.astype(jnp.float32).T, inverse.astype(jnp.float32).T, precision=highest
    )
    running = jnp.dot(running, linear_part, precision=highest)
    return (running, running)


def on_device(flow_state, forcing, tile_inverse, coupling, sweep_order):
    local_inst, resident_tiles, width = flow_state.shape
    period = lax.axis_size("inst") * local_inst
    my_rows = lax.axis_index("inst") * local_inst + jnp.arange(local_inst, dtype=jnp.int32)
    scale = spectral_gain / period
    inverse_seq = tile_inverse[sweep_order]
    couple_seq = coupling[sweep_order]
    identity_map = jnp.eye(width, dtype=jnp.float32)
    _, prefix_maps = lax.scan(compose_tile, identity_map, (inverse_seq, couple_seq))
    whole_map = prefix_maps[-1]
    zero_inflow = jnp.zeros((local_inst, width), jnp.float32)
    for repeat in range(ITERS):
        portion = lax.all_gather(flow_state, "inst", axis=0, tiled=True)
        col_ids = jnp.arange(portion.shape[0], dtype=jnp.int32)
        weights = spectral_rows(my_rows, col_ids, period)
        source_term = jnp.einsum("ij,jtb->itb", weights, portion, precision=highest)
        right_side = forcing - scale * source_term - flow_state
        ordered = jnp.swapaxes(right_side[:, sweep_order], 0, 1)
        _, local_part = lax.scan(visit_tile, zero_inflow, (ordered, inverse_seq, couple_seq))
        outflow_shift = local_part[-1]

        def advance(position, inflow):
            leaving = jnp.dot(inflow, whole_map, precision=highest) + outflow_shift
            return passed_along(leaving, "axial", 1)

        inflow = lax.fori_loop(0, lax.axis_size("axial") - 1, advance, zero_inflow)
        updates = local_part + jnp.einsum("ib,kbc->kic", inflow, prefix_maps, precision=highest)
        increment = jnp.zeros_like(flow_state).at[:, sweep_order].set(jnp.swapaxes(updates, 0, 1))
        flow_state = flow_state + increment
    return flow_state


def solution(mesh):
    return jax.shard_map(
        on_device,
        mesh=mesh,
        in_specs=(
            P("inst", "axial", None),
            P("inst", "axial", None),
            P("axial", None, None),
            P("axial", None, None),
            P("axial"),
        ),
        out_specs=P("inst", "axial", None),
        check_vma=False,
    )
```

profile of v0, /device:TPU:24, one launch (start us, length us, event | category | flops | bytes accessed | tf_op | source)
XLA Modules:
  0.0 710.0 jit_solution(3527732776291304235)
XLA Ops:
  11.0 13.7 %all_gather.6 = f32[32,16,320]{2,1,0:T(8,128)S(1)} all-gather(f32[4,16,320]{2,1,0:T(8,128)S(1)} %copy-done), channel_id=1, replica_groups=mesh['inst'=8,'axial'=32] {'inst'}, dimensions={0}, use_global_device_ids=true | all-gather | bytes 737280 | tf_op jit(solution)/shard_map/all_gather | solution.py:58
  26.2 40.5 %while.56 = (s32[]{:T(128)}, f32[4,320]{1,0:T(4,128)S(1)}, f32[16,4,320]{2,1,0:T(4,128)S(1)}, f32[16,4,320]{2,1,0:T(4,128)S(1)}, bf16[16,320,320]{2,1,0:T(8,128)(2,1)}, /*index=5*/bf16[16,320,320]{2,1,0:T(8,128)(2,1)}, s32[]{:T(128)}) while((s32[]{:T(128)}, f32[4,320]{1,0:T(4,128)S(1)}, f32[16,4,320]{2,1,0:T(4,128)S(1)}, ...), condition=%wide.region_1.2_spmd, body=%wide.region_0.1_spmd.sunk | while | flops 9831682 | bytes 527437 | solution.py:64
  66.8 56.5 %while.57 = (s32[]{:T(128)}, f32[320,320]{0,1:T(8,128)S(1)}, f32[16,320,320]{1,2,0:T(8,128)}, bf16[16,320,320]{2,1,0:T(8,128)(2,1)}, bf16[16,320,320]{2,1,0:T(8,128)(2,1)}, /*index=5*/s32[]{:T(128)}) while((s32[]{:T(128)}, f32[320,320]{0,1:T(8,128)S(1)}, f32[16,320,320]{1,2,0:T(8,128)}, bf16[16,320,320]{2,1,0:T(8,128)(2,1)}, ...), condition=%wide.region_3.4_spmd, body=%wide.region_2.3_spmd.sunk | while | flops 458854400 | bytes 3442245 | solution.py:54
  123.2 8.6 %copy.40 = f32[16,320,320]{2,1,0:T(8,128)} copy(f32[16,320,320]{1,2,0:T(8,128)} %get-tuple-element.141) | data formatting | bytes 13107200 | tf_op jit(solution)/shard_map/while | solution.py:54
  133.0 249.3 %while.58 = (s32[]{:T(128)}, f32[4,320]{1,0:T(4,128)S(1)}, f32[320,320]{1,0:T(8,128)S(1)}, f32[4,320]{1,0:T(4,128)S(1)}, s32[]{:T(128)}) while((s32[]{:T(128)}, f32[4,320]{1,0:T(4,128)S(1)}, f32[320,320]{1,0:T(8,128)S(1)}, f32[4,320]{1,0:T(4,128)S(1)}, s32[]{:T(128)}) %tuple.87), condition=%wide.region_5.6_spmd, body=%wide.region_4.5_spmd.sunk | while | flops 4916482 | bytes 445541 | solution.py:71
  137.2 5.7 collective-permute-done
  145.2 5.7 collective-permute-done
  153.1 5.7 collective-permute-done
  161.1 5.7 collective-permute-done
  169.1 5.7 collective-permute-done
  177.1 5.7 collective-permute-done
  185.0 5.7 collective-permute-done
  193.0 5.7 collective-permute-done
  201.0 5.7 collective-permute-done
  209.0 5.7 collective-permute-done
  217.0 5.7 collective-permute-done
  224.9 5.7 collective-permute-done
  232.9 5.7 collective-permute-done
  240.9 5.7 collective-permute-done
  248.9 5.7 collective-permute-done
  256.9 5.7 collective-permute-done
  264.8 5.7 collective-permute-done
  272.8 5.7 collective-permute-done
  280.8 5.7 collective-permute-done
  288.8 5.7 collective-permute-done
  296.8 5.7 collective-permute-done
  304.7 5.7 collective-permute-done
  312.7 5.7 collective-permute-done
  320.7 5.7 collective-permute-done
  328.7 5.7 collective-permute-done
  336.7 5.7 collective-permute-done
  344.6 5.7 collective-permute-done
  368.6 5.7 collective-permute-done
  382.3 11.0 %fusion.22 = f32[16,4,320]{2,1,0:T(4,128)S(1)} fusion(f32[16,4,320]{2,1,0:T(4,128)S(1)} %get-tuple-element.140, f32[16,320,320]{1,2,0:T(8,128)} %get-tuple-element.141, f32[4,320]{1,0:T(4,128)S(1)} %get-tuple-element.142), kind=kOutput, calls=%fused_computation.38 | convolution fusion | flops 78663680 | bytes 6722560 | tf_op jit(solution)/shard_map/ib,kbc->kic/dot_general | solution.py:72
  394.3 13.6 %all_gather.7 = f32[32,16,320]{2,1,0:T(8,128)S(1)} all-gather(f32[4,16,320]{2,1,0:T(8,128)S(1)} %copy_add_fusion.1), channel_id=1, replica_groups=mesh['inst'=8,'axial'=32] {'inst'}, dimensions={0}, use_global_device_ids=true | all-gather | bytes 737280 | tf_op jit(solution)/shard_map/all_gather | solution.py:58
  409.4 40.5 %while.59 = (s32[]{:T(128)}, f32[4,320]{1,0:T(4,128)S(1)}, f32[16,4,320]{2,1,0:T(4,128)S(1)}, f32[16,4,320]{2,1,0:T(4,128)S(1)}, bf16[16,320,320]{2,1,0:T(8,128)(2,1)}, /*index=5*/bf16[16,320,320]{2,1,0:T(8,128)(2,1)}, s32[]{:T(128)}) while((s32[]{:T(128)}, f32[4,320]{1,0:T(4,128)S(1)}, f32[16,4,320]{2,1,0:T(4,128)S(1)}, ...), condition=%wide.region_8.9_spmd, body=%wide.region_7.8_spmd.sunk | while | flops 9831682 | bytes 527437 | solution.py:64
  449.9 247.4 %while.60 = (s32[]{:T(128)}, f32[4,320]{1,0:T(4,128)S(1)}, f32[320,320]{1,0:T(8,128)S(1)}, f32[4,320]{1,0:T(4,128)S(1)}, s32[]{:T(128)}) while((s32[]{:T(128)}, f32[4,320]{1,0:T(4,128)S(1)}, f32[320,320]{1,0:T(8,128)S(1)}, f32[4,320]{1,0:T(4,128)S(1)}, s32[]{:T(128)}) %tuple.96), condition=%wide.region_10.11_spmd, body=%wide.region_9.10_spmd.sunk | while | flops 4916482 | bytes 445541 | solution.py:71
  460.2 5.7 collective-permute-done.1
  484.1 5.7 collective-permute-done.1
  508.1 5.7 collective-permute-done.1
  532.0 5.7 collective-permute-done.1
  563.9 5.7 collective-permute-done.1
  587.9 5.7 collective-permute-done.1
  611.8 5.7 collective-permute-done.1
  635.8 5.7 collective-permute-done.1
  659.7 5.7 collective-permute-done.1
  683.6 5.7 collective-permute-done.1
  697.3 11.0 %fusion.21 = f32[16,4,320]{2,1,0:T(4,128)S(1)} fusion(f32[16,4,320]{2,1,0:T(4,128)S(1)} %get-tuple-element.143, f32[16,320,320]{1,2,0:T(8,128)} %get-tuple-element.141, f32[4,320]{1,0:T(4,128)S(1)} %get-tuple-element.144), kind=kOutput, calls=%fused_computation.36 | convolution fusion | flops 78663680 | bytes 6722560 | tf_op jit(solution)/shard_map/ib,kbc->kic/dot_general | solution.py:72
  (294 shorter events, 433.5 us)
Async XLA Ops:
  133.3 9.6 %collective-permute-start = (f32[4,320]{1,0:T(4,128)S(1)}, f32[4,320]{1,0:T(4,128)S(1)}, u32[]{:S(2)}, u32[]{:S(2)}) collective-permute-start(f32[4,320]{1,0:T(4,128)S(1)} %convolution_add_fusion.4), channel_id=1, source_target_pairs={{0,1},{1,2},{2,3},{3,4},{4,5},{5,6},{6,7},{7,8},{8,9},{9,10},{10,1... | collective-permute-start | bytes 15368 | tf_op jit(solution)/shard_map/while/body/eval_jaxpr/ppermute | solution.py:16
  143.2 7.6 %collective-permute-start = (f32[4,320]{1,0:T(4,128)S(1)}, f32[4,320]{1,0:T(4,128)S(1)}, u32[]{:S(2)}, u32[]{:S(2)}) collective-permute-start(f32[4,320]{1,0:T(4,128)S(1)} %convolution_add_fusion.4), channel_id=1, source_target_pairs={{0,1},{1,2},{2,3},{3,4},{4,5},{5,6},{6,7},{7,8},{8,9},{9,10},{10,1... | collective-permute-start | bytes 15368 | tf_op jit(solution)/shard_map/while/body/eval_jaxpr/ppermute | solution.py:16
  151.2 7.6 %collective-permute-start = (f32[4,320]{1,0:T(4,128)S(1)}, f32[4,320]{1,0:T(4,128)S(1)}, u32[]{:S(2)}, u32[]{:S(2)}) collective-permute-start(f32[4,320]{1,0:T(4,128)S(1)} %convolution_add_fusion.4), channel_id=1, source_target_pairs={{0,1},{1,2},{2,3},{3,4},{4,5},{5,6},{6,7},{7,8},{8,9},{9,10},{10,1... | collective-permute-start | bytes 15368 | tf_op jit(solution)/shard_map/while/body/eval_jaxpr/ppermute | solution.py:16
  159.2 7.6 %collective-permute-start = (f32[4,320]{1,0:T(4,128)S(1)}, f32[4,320]{1,0:T(4,128)S(1)}, u32[]{:S(2)}, u32[]{:S(2)}) collective-permute-start(f32[4,320]{1,0:T(4,128)S(1)} %convolution_add_fusion.4), channel_id=1, source_target_pairs={{0,1},{1,2},{2,3},{3,4},{4,5},{5,6},{6,7},{7,8},{8,9},{9,10},{10,1... | collective-permute-start | bytes 15368 | tf_op jit(solution)/shard_map/while/body/eval_jaxpr/ppermute | solution.py:16
  167.1 7.6 %collective-permute-start = (f32[4,320]{1,0:T(4,128)S(1)}, f32[4,320]{1,0:T(4,128)S(1)}, u32[]{:S(2)}, u32[]{:S(2)}) collective-permute-start(f32[4,320]{1,0:T(4,128)S(1)} %convolution_add_fusion.4), channel_id=1, source_target_pairs={{0,1},{1,2},{2,3},{3,4},{4,5},{5,6},{6,7},{7,8},{8,9},{9,10},{10,1... | collective-permute-start | bytes 15368 | tf_op jit(solution)/shard_map/while/body/eval_jaxpr/ppermute | solution.py:16
  175.1 7.6 %collective-permute-start = (f32[4,320]{1,0:T(4,128)S(1)}, f32[4,320]{1,0:T(4,128)S(1)}, u32[]{:S(2)}, u32[]{:S(2)}) collective-permute-start(f32[4,320]{1,0:T(4,128)S(1)} %convolution_add_fusion.4), channel_id=1, source_target_pairs={{0,1},{1,2},{2,3},{3,4},{4,5},{5,6},{6,7},{7,8},{8,9},{9,10},{10,1... | collective-permute-start | bytes 15368 | tf_op jit(solution)/shard_map/while/body/eval_jaxpr/ppermute | solution.py:16
  183.1 7.6 %collective-permute-start = (f32[4,320]{1,0:T(4,128)S(1)}, f32[4,320]{1,0:T(4,128)S(1)}, u32[]{:S(2)}, u32[]{:S(2)}) collective-permute-start(f32[4,320]{1,0:T(4,128)S(1)} %convolution_add_fusion.4), channel_id=1, source_target_pairs={{0,1},{1,2},{2,3},{3,4},{4,5},{5,6},{6,7},{7,8},{8,9},{9,10},{10,1... | collective-permute-start | bytes 15368 | tf_op jit(solution)/shard_map/while/body/eval_jaxpr/ppermute | solution.py:16
  191.1 7.6 %collective-permute-start = (f32[4,320]{1,0:T(4,128)S(1)}, f32[4,320]{1,0:T(4,128)S(1)}, u32[]{:S(2)}, u32[]{:S(2)}) collective-permute-start(f32[4,320]{1,0:T(4,128)S(1)} %convolution_add_fusion.4), channel_id=1, source_target_pairs={{0,1},{1,2},{2,3},{3,4},{4,5},{5,6},{6,7},{7,8},{8,9},{9,10},{10,1... | collective-permute-start | bytes 15368 | tf_op jit(solution)/shard_map/while/body/eval_jaxpr/ppermute | solution.py:16
  199.1 7.6 %collective-permute-start = (f32[4,320]{1,0:T(4,128)S(1)}, f32[4,320]{1,0:T(4,128)S(1)}, u32[]{:S(2)}, u32[]{:S(2)}) collective-permute-start(f32[4,320]{1,0:T(4,128)S(1)} %convolution_add_fusion.4), channel_id=1, source_target_pairs={{0,1},{1,2},{2,3},{3,4},{4,5},{5,6},{6,7},{7,8},{8,9},{9,10},{10,1... | collective-permute-start | bytes 15368 | tf_op jit(solution)/shard_map/while/body/eval_jaxpr/ppermute | solution.py:16
  207.0 7.6 %collective-permute-start = (f32[4,320]{1,0:T(4,128)S(1)}, f32[4,320]{1,0:T(4,128)S(1)}, u32[]{:S(2)}, u32[]{:S(2)}) collective-permute-start(f32[4,320]{1,0:T(4,128)S(1)} %convolution_add_fusion.4), channel_id=1, source_target_pairs={{0,1},{1,2},{2,3},{3,4},{4,5},{5,6},{6,7},{7,8},{8,9},{9,10},{10,1... | collective-permute-start | bytes 15368 | tf_op jit(solution)/shard_map/while/body/eval_jaxpr/ppermute | solution.py:16
  215.0 7.6 %collective-permute-start = (f32[4,320]{1,0:T(4,128)S(1)}, f32[4,320]{1,0:T(4,128)S(1)}, u32[]{:S(2)}, u32[]{:S(2)}) collective-permute-start(f32[4,320]{1,0:T(4,128)S(1)} %convolution_add_fusion.4), channel_id=1, source_target_pairs={{0,1},{1,2},{2,3},{3,4},{4,5},{5,6},{6,7},{7,8},{8,9},{9,10},{10,1... | collective-permute-start | bytes 15368 | tf_op jit(solution)/shard_map/while/body/eval_jaxpr/ppermute | solution.py:16
  223.0 7.6 %collective-permute-start = (f32[4,320]{1,0:T(4,128)S(1)}, f32[4,320]{1,0:T(4,128)S(1)}, u32[]{:S(2)}, u32[]{:S(2)}) collective-permute-start(f32[4,320]{1,0:T(4,128)S(1)} %convolution_add_fusion.4), channel_id=1, source_target_pairs={{0,1},{1,2},{2,3},{3,4},{4,5},{5,6},{6,7},{7,8},{8,9},{9,10},{10,1... | collective-permute-start | bytes 15368 | tf_op jit(solution)/shard_map/while/body/eval_jaxpr/ppermute | solution.py:16
  231.0 7.6 %collective-permute-start = (f32[4,320]{1,0:T(4,128)S(1)}, f32[4,320]{1,0:T(4,128)S(1)}, u32[]{:S(2)}, u32[]{:S(2)}) collective-permute-start(f32[4,320]{1,0:T(4,128)S(1)} %convolution_add_fusion.4), channel_id=1, source_target_pairs={{0,1},{1,2},{2,3},{3,4},{4,5},{5,6},{6,7},{7,8},{8,9},{9,10},{10,1... | collective-permute-start | bytes 15368 | tf_op jit(solution)/shard_map/while/body/eval_jaxpr/ppermute | solution.py:16
  239.0 7.6 %collective-permute-start = (f32[4,320]{1,0:T(4,128)S(1)}, f32[4,320]{1,0:T(4,128)S(1)}, u32[]{:S(2)}, u32[]{:S(2)}) collective-permute-start(f32[4,320]{1,0:T(4,128)S(1)} %convolution_add_fusion.4), channel_id=1, source_target_pairs={{0,1},{1,2},{2,3},{3,4},{4,5},{5,6},{6,7},{7,8},{8,9},{9,10},{10,1... | collective-permute-start | bytes 15368 | tf_op jit(solution)/shard_map/while/body/eval_jaxpr/ppermute | solution.py:16
  254.9 7.6 %collective-permute-start = (f32[4,320]{1,0:T(4,128)S(1)}, f32[4,320]{1,0:T(4,128)S(1)}, u32[]{:S(2)}, u32[]{:S(2)}) collective-permute-start(f32[4,320]{1,0:T(4,128)S(1)} %convolution_add_fusion.4), channel_id=1, source_target_pairs={{0,1},{1,2},{2,3},{3,4},{4,5},{5,6},{6,7},{7,8},{8,9},{9,10},{10,1... | collective-permute-start | bytes 15368 | tf_op jit(solution)/shard_map/while/body/eval_jaxpr/ppermute | solution.py:16
  262.9 7.6 %collective-permute-start = (f32[4,320]{1,0:T(4,128)S(1)}, f32[4,320]{1,0:T(4,128)S(1)}, u32[]{:S(2)}, u32[]{:S(2)}) collective-permute-start(f32[4,320]{1,0:T(4,128)S(1)} %convolution_add_fusion.4), channel_id=1, source_target_pairs={{0,1},{1,2},{2,3},{3,4},{4,5},{5,6},{6,7},{7,8},{8,9},{9,10},{10,1... | collective-permute-start | bytes 15368 | tf_op jit(solution)/shard_map/while/body/eval_jaxpr/ppermute | solution.py:16
  278.9 7.6 %collective-permute-start = (f32[4,320]{1,0:T(4,128)S(1)}, f32[4,320]{1,0:T(4,128)S(1)}, u32[]{:S(2)}, u32[]{:S(2)}) collective-permute-start(f32[4,320]{1,0:T(4,128)S(1)} %convolution_add_fusion.4), channel_id=1, source_target_pairs={{0,1},{1,2},{2,3},{3,4},{4,5},{5,6},{6,7},{7,8},{8,9},{9,10},{10,1... | collective-permute-start | bytes 15368 | tf_op jit(solution)/shard_map/while/body/eval_jaxpr/ppermute | solution.py:16
  286.8 7.6 %collective-permute-start = (f32[4,320]{1,0:T(4,128)S(1)}, f32[4,320]{1,0:T(4,128)S(1)}, u32[]{:S(2)}, u32[]{:S(2)}) collective-permute-start(f32[4,320]{1,0:T(4,128)S(1)} %convolution_add_fusion.4), channel_id=1, source_target_pairs={{0,1},{1,2},{2,3},{3,4},{4,5},{5,6},{6,7},{7,8},{8,9},{9,10},{10,1... | collective-permute-start | bytes 15368 | tf_op jit(solution)/shard_map/while/body/eval_jaxpr/ppermute | solution.py:16
  302.8 7.6 %collective-permute-start = (f32[4,320]{1,0:T(4,128)S(1)}, f32[4,320]{1,0:T(4,128)S(1)}, u32[]{:S(2)}, u32[]{:S(2)}) collective-permute-start(f32[4,320]{1,0:T(4,128)S(1)} %convolution_add_fusion.4), channel_id=1, source_target_pairs={{0,1},{1,2},{2,3},{3,4},{4,5},{5,6},{6,7},{7,8},{8,9},{9,10},{10,1... | collective-permute-start | bytes 15368 | tf_op jit(solution)/shard_map/while/body/eval_jaxpr/ppermute | solution.py:16
  310.8 7.6 %collective-permute-start = (f32[4,320]{1,0:T(4,128)S(1)}, f32[4,320]{1,0:T(4,128)S(1)}, u32[]{:S(2)}, u32[]{:S(2)}) collective-permute-start(f32[4,320]{1,0:T(4,128)S(1)} %convolution_add_fusion.4), channel_id=1, source_target_pairs={{0,1},{1,2},{2,3},{3,4},{4,5},{5,6},{6,7},{7,8},{8,9},{9,10},{10,1... | collective-permute-start | bytes 15368 | tf_op jit(solution)/shard_map/while/body/eval_jaxpr/ppermute | solution.py:16
  318.8 7.6 %collective-permute-start = (f32[4,320]{1,0:T(4,128)S(1)}, f32[4,320]{1,0:T(4,128)S(1)}, u32[]{:S(2)}, u32[]{:S(2)}) collective-permute-start(f32[4,320]{1,0:T(4,128)S(1)} %convolution_add_fusion.4), channel_id=1, source_target_pairs={{0,1},{1,2},{2,3},{3,4},{4,5},{5,6},{6,7},{7,8},{8,9},{9,10},{10,1... | collective-permute-start | bytes 15368 | tf_op jit(solution)/shard_map/while/body/eval_jaxpr/ppermute | solution.py:16
  326.7 7.6 %collective-permute-start = (f32[4,320]{1,0:T(4,128)S(1)}, f32[4,320]{1,0:T(4,128)S(1)}, u32[]{:S(2)}, u32[]{:S(2)}) collective-permute-start(f32[4,320]{1,0:T(4,128)S(1)} %convolution_add_fusion.4), channel_id=1, source_target_pairs={{0,1},{1,2},{2,3},{3,4},{4,5},{5,6},{6,7},{7,8},{8,9},{9,10},{10,1... | collective-permute-start | bytes 15368 | tf_op jit(solution)/shard_map/while/body/eval_jaxpr/ppermute | solution.py:16
  334.7 7.6 %collective-permute-start = (f32[4,320]{1,0:T(4,128)S(1)}, f32[4,320]{1,0:T(4,128)S(1)}, u32[]{:S(2)}, u32[]{:S(2)}) collective-permute-start(f32[4,320]{1,0:T(4,128)S(1)} %convolution_add_fusion.4), channel_id=1, source_target_pairs={{0,1},{1,2},{2,3},{3,4},{4,5},{5,6},{6,7},{7,8},{8,9},{9,10},{10,1... | collective-permute-start | bytes 15368 | tf_op jit(solution)/shard_map/while/body/eval_jaxpr/ppermute | solution.py:16
  342.7 7.6 %collective-permute-start = (f32[4,320]{1,0:T(4,128)S(1)}, f32[4,320]{1,0:T(4,128)S(1)}, u32[]{:S(2)}, u32[]{:S(2)}) collective-permute-start(f32[4,320]{1,0:T(4,128)S(1)} %convolution_add_fusion.4), channel_id=1, source_target_pairs={{0,1},{1,2},{2,3},{3,4},{4,5},{5,6},{6,7},{7,8},{8,9},{9,10},{10,1... | collective-permute-start | bytes 15368 | tf_op jit(solution)/shard_map/while/body/eval_jaxpr/ppermute | solution.py:16
  358.6 7.6 %collective-permute-start = (f32[4,320]{1,0:T(4,128)S(1)}, f32[4,320]{1,0:T(4,128)S(1)}, u32[]{:S(2)}, u32[]{:S(2)}) collective-permute-start(f32[4,320]{1,0:T(4,128)S(1)} %convolution_add_fusion.4), channel_id=1, source_target_pairs={{0,1},{1,2},{2,3},{3,4},{4,5},{5,6},{6,7},{7,8},{8,9},{9,10},{10,1... | collective-permute-start | bytes 15368 | tf_op jit(solution)/shard_map/while/body/eval_jaxpr/ppermute | solution.py:16
  366.6 7.6 %collective-permute-start = (f32[4,320]{1,0:T(4,128)S(1)}, f32[4,320]{1,0:T(4,128)S(1)}, u32[]{:S(2)}, u32[]{:S(2)}) collective-permute-start(f32[4,320]{1,0:T(4,128)S(1)} %convolution_add_fusion.4), channel_id=1, source_target_pairs={{0,1},{1,2},{2,3},{3,4},{4,5},{5,6},{6,7},{7,8},{8,9},{9,10},{10,1... | collective-permute-start | bytes 15368 | tf_op jit(solution)/shard_map/while/body/eval_jaxpr/ppermute | solution.py:16
  450.3 7.6 %collective-permute-start.1 = (f32[4,320]{1,0:T(4,128)S(1)}, f32[4,320]{1,0:T(4,128)S(1)}, u32[]{:S(2)}, u32[]{:S(2)}) collective-permute-start(f32[4,320]{1,0:T(4,128)S(1)} %convolution_add_fusion.5), channel_id=1, source_target_pairs={{0,1},{1,2},{2,3},{3,4},{4,5},{5,6},{6,7},{7,8},{8,9},{9,10},{10,1... | collective-permute-start | bytes 15368 | tf_op jit(solution)/shard_map/while/body/eval_jaxpr/ppermute | solution.py:16
  458.3 7.6 %collective-permute-start.1 = (f32[4,320]{1,0:T(4,128)S(1)}, f32[4,320]{1,0:T(4,128)S(1)}, u32[]{:S(2)}, u32[]{:S(2)}) collective-permute-start(f32[4,320]{1,0:T(4,128)S(1)} %convolution_add_fusion.5), channel_id=1, source_target_pairs={{0,1},{1,2},{2,3},{3,4},{4,5},{5,6},{6,7},{7,8},{8,9},{9,10},{10,1... | collective-permute-start | bytes 15368 | tf_op jit(solution)/shard_map/while/body/eval_jaxpr/ppermute | solution.py:16
  474.2 7.6 %collective-permute-start.1 = (f32[4,320]{1,0:T(4,128)S(1)}, f32[4,320]{1,0:T(4,128)S(1)}, u32[]{:S(2)}, u32[]{:S(2)}) collective-permute-start(f32[4,320]{1,0:T(4,128)S(1)} %convolution_add_fusion.5), channel_id=1, source_target_pairs={{0,1},{1,2},{2,3},{3,4},{4,5},{5,6},{6,7},{7,8},{8,9},{9,10},{10,1... | collective-permute-start | bytes 15368 | tf_op jit(solution)/shard_map/while/body/eval_jaxpr/ppermute | solution.py:16
  482.2 7.6 %collective-permute-start.1 = (f32[4,320]{1,0:T(4,128)S(1)}, f32[4,320]{1,0:T(4,128)S(1)}, u32[]{:S(2)}, u32[]{:S(2)}) collective-permute-start(f32[4,320]{1,0:T(4,128)S(1)} %convolution_add_fusion.5), channel_id=1, source_target_pairs={{0,1},{1,2},{2,3},{3,4},{4,5},{5,6},{6,7},{7,8},{8,9},{9,10},{10,1... | collective-permute-start | bytes 15368 | tf_op jit(solution)/shard_map/while/body/eval_jaxpr/ppermute | solution.py:16
  498.2 7.6 %collective-permute-start.1 = (f32[4,320]{1,0:T(4,128)S(1)}, f32[4,320]{1,0:T(4,128)S(1)}, u32[]{:S(2)}, u32[]{:S(2)}) collective-permute-start(f32[4,320]{1,0:T(4,128)S(1)} %convolution_add_fusion.5), channel_id=1, source_target_pairs={{0,1},{1,2},{2,3},{3,4},{4,5},{5,6},{6,7},{7,8},{8,9},{9,10},{10,1... | collective-permute-start | bytes 15368 | tf_op jit(solution)/shard_map/while/body/eval_jaxpr/ppermute | solution.py:16
  506.1 7.6 %collective-permute-start.1 = (f32[4,320]{1,0:T(4,128)S(1)}, f32[4,320]{1,0:T(4,128)S(1)}, u32[]{:S(2)}, u32[]{:S(2)}) collective-permute-start(f32[4,320]{1,0:T(4,128)S(1)} %convolution_add_fusion.5), channel_id=1, source_target_pairs={{0,1},{1,2},{2,3},{3,4},{4,5},{5,6},{6,7},{7,8},{8,9},{9,10},{10,1... | collective-permute-start | bytes 15368 | tf_op jit(solution)/shard_map/while/body/eval_jaxpr/ppermute | solution.py:16
  522.1 7.6 %collective-permute-start.1 = (f32[4,320]{1,0:T(4,128)S(1)}, f32[4,320]{1,0:T(4,128)S(1)}, u32[]{:S(2)}, u32[]{:S(2)}) collective-permute-start(f32[4,320]{1,0:T(4,128)S(1)} %convolution_add_fusion.5), channel_id=1, source_target_pairs={{0,1},{1,2},{2,3},{3,4},{4,5},{5,6},{6,7},{7,8},{8,9},{9,10},{10,1... | collective-permute-start | bytes 15368 | tf_op jit(solution)/shard_map/while/body/eval_jaxpr/ppermute | solution.py:16
  530.1 7.6 %collective-permute-start.1 = (f32[4,320]{1,0:T(4,128)S(1)}, f32[4,320]{1,0:T(4,128)S(1)}, u32[]{:S(2)}, u32[]{:S(2)}) collective-permute-start(f32[4,320]{1,0:T(4,128)S(1)} %convolution_add_fusion.5), channel_id=1, source_target_pairs={{0,1},{1,2},{2,3},{3,4},{4,5},{5,6},{6,7},{7,8},{8,9},{9,10},{10,1... | collective-permute-start | bytes 15368 | tf_op jit(solution)/shard_map/while/body/eval_jaxpr/ppermute | solution.py:16
  546.0 7.6 %collective-permute-start.1 = (f32[4,320]{1,0:T(4,128)S(1)}, f32[4,320]{1,0:T(4,128)S(1)}, u32[]{:S(2)}, u32[]{:S(2)}) collective-permute-start(f32[4,320]{1,0:T(4,128)S(1)} %convolution_add_fusion.5), channel_id=1, source_target_pairs={{0,1},{1,2},{2,3},{3,4},{4,5},{5,6},{6,7},{7,8},{8,9},{9,10},{10,1... | collective-permute-start | bytes 15368 | tf_op jit(solution)/shard_map/while/body/eval_jaxpr/ppermute | solution.py:16
  554.0 7.6 %collective-permute-start.1 = (f32[4,320]{1,0:T(4,128)S(1)}, f32[4,320]{1,0:T(4,128)S(1)}, u32[]{:S(2)}, u32[]{:S(2)}) collective-permute-start(f32[4,320]{1,0:T(4,128)S(1)} %convolution_add_fusion.5), channel_id=1, source_target_pairs={{0,1},{1,2},{2,3},{3,4},{4,5},{5,6},{6,7},{7,8},{8,9},{9,10},{10,1... | collective-permute-start | bytes 15368 | tf_op jit(solution)/shard_map/while/body/eval_jaxpr/ppermute | solution.py:16
  562.0 7.6 %collective-permute-start.1 = (f32[4,320]{1,0:T(4,128)S(1)}, f32[4,320]{1,0:T(4,128)S(1)}, u32[]{:S(2)}, u32[]{:S(2)}) collective-permute-start(f32[4,320]{1,0:T(4,128)S(1)} %convolution_add_fusion.5), channel_id=1, source_target_pairs={{0,1},{1,2},{2,3},{3,4},{4,5},{5,6},{6,7},{7,8},{8,9},{9,10},{10,1... | collective-permute-start | bytes 15368 | tf_op jit(solution)/shard_map/while/body/eval_jaxpr/ppermute | solution.py:16
  570.0 7.6 %collective-permute-start.1 = (f32[4,320]{1,0:T(4,128)S(1)}, f32[4,320]{1,0:T(4,128)S(1)}, u32[]{:S(2)}, u32[]{:S(2)}) collective-permute-start(f32[4,320]{1,0:T(4,128)S(1)} %convolution_add_fusion.5), channel_id=1, source_target_pairs={{0,1},{1,2},{2,3},{3,4},{4,5},{5,6},{6,7},{7,8},{8,9},{9,10},{10,1... | collective-permute-start | bytes 15368 | tf_op jit(solution)/shard_map/while/body/eval_jaxpr/ppermute | solution.py:16
  578.0 7.6 %collective-permute-start.1 = (f32[4,320]{1,0:T(4,128)S(1)}, f32[4,320]{1,0:T(4,128)S(1)}, u32[]{:S(2)}, u32[]{:S(2)}) collective-permute-start(f32[4,320]{1,0:T(4,128)S(1)} %convolution_add_fusion.5), channel_id=1, source_target_pairs={{0,1},{1,2},{2,3},{3,4},{4,5},{5,6},{6,7},{7,8},{8,9},{9,10},{10,1... | collective-permute-start | bytes 15368 | tf_op jit(solution)/shard_map/while/body/eval_jaxpr/ppermute | solution.py:16
  585.9 7.6 %collective-permute-start.1 = (f32[4,320]{1,0:T(4,128)S(1)}, f32[4,320]{1,0:T(4,128)S(1)}, u32[]{:S(2)}, u32[]{:S(2)}) collective-permute-start(f32[4,320]{1,0:T(4,128)S(1)} %convolution_add_fusion.5), channel_id=1, source_target_pairs={{0,1},{1,2},{2,3},{3,4},{4,5},{5,6},{6,7},{7,8},{8,9},{9,10},{10,1... | collective-permute-start | bytes 15368 | tf_op jit(solution)/shard_map/while/body/eval_jaxpr/ppermute | solution.py:16
  601.9 7.6 %collective-permute-start.1 = (f32[4,320]{1,0:T(4,128)S(1)}, f32[4,320]{1,0:T(4,128)S(1)}, u32[]{:S(2)}, u32[]{:S(2)}) collective-permute-start(f32[4,320]{1,0:T(4,128)S(1)} %convolution_add_fusion.5), channel_id=1, source_target_pairs={{0,1},{1,2},{2,3},{3,4},{4,5},{5,6},{6,7},{7,8},{8,9},{9,10},{10,1... | collective-permute-start | bytes 15368 | tf_op jit(solution)/shard_map/while/body/eval_jaxpr/ppermute | solution.py:16
  609.9 7.6 %collective-permute-start.1 = (f32[4,320]{1,0:T(4,128)S(1)}, f32[4,320]{1,0:T(4,128)S(1)}, u32[]{:S(2)}, u32[]{:S(2)}) collective-permute-start(f32[4,320]{1,0:T(4,128)S(1)} %convolution_add_fusion.5), channel_id=1, source_target_pairs={{0,1},{1,2},{2,3},{3,4},{4,5},{5,6},{6,7},{7,8},{8,9},{9,10},{10,1... | collective-permute-start | bytes 15368 | tf_op jit(solution)/shard_map/while/body/eval_jaxpr/ppermute | solution.py:16
  625.8 7.6 %collective-permute-start.1 = (f32[4,320]{1,0:T(4,128)S(1)}, f32[4,320]{1,0:T(4,128)S(1)}, u32[]{:S(2)}, u32[]{:S(2)}) collective-permute-start(f32[4,320]{1,0:T(4,128)S(1)} %convolution_add_fusion.5), channel_id=1, source_target_pairs={{0,1},{1,2},{2,3},{3,4},{4,5},{5,6},{6,7},{7,8},{8,9},{9,10},{10,1... | collective-permute-start | bytes 15368 | tf_op jit(solution)/shard_map/while/body/eval_jaxpr/ppermute | solution.py:16
  633.8 7.6 %collective-permute-start.1 = (f32[4,320]{1,0:T(4,128)S(1)}, f32[4,320]{1,0:T(4,128)S(1)}, u32[]{:S(2)}, u32[]{:S(2)}) collective-permute-start(f32[4,320]{1,0:T(4,128)S(1)} %convolution_add_fusion.5), channel_id=1, source_target_pairs={{0,1},{1,2},{2,3},{3,4},{4,5},{5,6},{6,7},{7,8},{8,9},{9,10},{10,1... | collective-permute-start | bytes 15368 | tf_op jit(solution)/shard_map/while/body/eval_jaxpr/ppermute | solution.py:16
  649.8 7.6 %collective-permute-start.1 = (f32[4,320]{1,0:T(4,128)S(1)}, f32[4,320]{1,0:T(4,128)S(1)}, u32[]{:S(2)}, u32[]{:S(2)}) collective-permute-start(f32[4,320]{1,0:T(4,128)S(1)} %convolution_add_fusion.5), channel_id=1, source_target_pairs={{0,1},{1,2},{2,3},{3,4},{4,5},{5,6},{6,7},{7,8},{8,9},{9,10},{10,1... | collective-permute-start | bytes 15368 | tf_op jit(solution)/shard_map/while/body/eval_jaxpr/ppermute | solution.py:16
  657.7 7.6 %collective-permute-start.1 = (f32[4,320]{1,0:T(4,128)S(1)}, f32[4,320]{1,0:T(4,128)S(1)}, u32[]{:S(2)}, u32[]{:S(2)}) collective-permute-start(f32[4,320]{1,0:T(4,128)S(1)} %convolution_add_fusion.5), channel_id=1, source_target_pairs={{0,1},{1,2},{2,3},{3,4},{4,5},{5,6},{6,7},{7,8},{8,9},{9,10},{10,1... | collective-permute-start | bytes 15368 | tf_op jit(solution)/shard_map/while/body/eval_jaxpr/ppermute | solution.py:16
  673.7 7.6 %collective-permute-start.1 = (f32[4,320]{1,0:T(4,128)S(1)}, f32[4,320]{1,0:T(4,128)S(1)}, u32[]{:S(2)}, u32[]{:S(2)}) collective-permute-start(f32[4,320]{1,0:T(4,128)S(1)} %convolution_add_fusion.5), channel_id=1, source_target_pairs={{0,1},{1,2},{2,3},{3,4},{4,5},{5,6},{6,7},{7,8},{8,9},{9,10},{10,1... | collective-permute-start | bytes 15368 | tf_op jit(solution)/shard_map/while/body/eval_jaxpr/ppermute | solution.py:16
  681.7 7.6 %collective-permute-start.1 = (f32[4,320]{1,0:T(4,128)S(1)}, f32[4,320]{1,0:T(4,128)S(1)}, u32[]{:S(2)}, u32[]{:S(2)}) collective-permute-start(f32[4,320]{1,0:T(4,128)S(1)} %convolution_add_fusion.5), channel_id=1, source_target_pairs={{0,1},{1,2},{2,3},{3,4},{4,5},{5,6},{6,7},{7,8},{8,9},{9,10},{10,1... | collective-permute-start | bytes 15368 | tf_op jit(solution)/shard_map/while/body/eval_jaxpr/ppermute | solution.py:16
  (16 other events, 131.9 us)
where the time goes:
time: 714 us; the launch traced here: 710 us
  waiting for transfers between devices  353 us (49%)
  matrix products  180 us (25%)
  starting transfers between devices  122 us (17%)
  blocking collectives  27.3 us (4%)
  local copies, waits for them, and re-layouts  24.1 us (3%)
    ppermute x62, waiting for transfers between devices, passed_along(): lax.ppermute(value, axis, [(source, source + steps) for source in range(l...  353 us
    ppermute x62, starting transfers between devices, passed_along(): lax.ppermute(value, axis, [(source, source + steps) for source in range(l...  122 us
    dot_general x32, matrix products, visit_tile(): jnp.dot(collapsed_result, inverse.astype(jnp.float32).T, precision=highest)  40.6 us
    dot_general x32, matrix products, visit_tile(): jnp.dot(upstream, couple_tile.astype(jnp.float32).T, precision=highest)  40.3 us
    dot_general x16, matrix products, compose_tile(): running = jnp.dot(running, linear_part, precision=highest)  33 us
    all_gather x2, blocking collectives, on_device(): portion = lax.all_gather(flow_state, 'inst', axis=0, tiled=True)  27.3 us
    dot_general x16, matrix products, compose_tile(): jnp.dot(couple_tile.astype(jnp.float32).T, inverse.astype(jnp.float32).T,...  22.7 us
    dot_general x2, matrix products, on_device(): jnp.einsum('ib,kbc->kic', inflow, prefix_maps, precision=highest)  21.9 us
  transfers between devices with their start and end apart: 62, of which 62 were waited for; matrix products, arithmetic and copies ran while one was open for 0% of the time, Pallas kernels for 0%

commit v1 on v0

v1 whole, which is shorter than its diff:
```python
import functools

import jax
import jax.numpy as jnp
import numpy as np
from jax import lax
from jax.experimental import pallas as pl
from jax.experimental.pallas import tpu as pltpu
from jax.sharding import PartitionSpec as P

ITERS = 2
SPECTRAL_GAIN = 2.0
MESH = pl.DeviceIdType.MESH
F32, BF16 = jnp.float32, jnp.bfloat16
NT = (((1,), (1,)), ((), ()))
NN = (((1,), (0,)), ((), ()))


def exchange_matrix(period, groups):
    idx = np.arange(period)
    dist = idx[:, None] - idx[None, :]
    angle = np.pi * dist / period
    safe = np.where(dist == 0, 1.0, np.sin(angle))
    deriv = np.where(dist == 0, 0.0, 0.5 * (1.0 - 2.0 * (dist % 2)) * np.cos(angle) / safe)
    e = deriv * (SPECTRAL_GAIN / period) + np.eye(period)
    whole = np.block([[-e @ e, e], [-2.0 * e, 2.0 * np.eye(period)]])
    local = period // groups
    perm = np.array(
        [part * period + dev * local + n for dev in range(groups) for part in range(2) for n in range(local)]
    )
    return whole[np.ix_(perm, perm)].astype(np.float32)


def halves(x):
    high = x.astype(BF16)
    low = (x - high.astype(F32)).astype(BF16)
    return high, low


def times(x, w, dims=NT):
    m = x.shape[0]
    y = lax.dot_general(jnp.concatenate(halves(x), 0), w, dims, preferred_element_type=F32)
    return y[:m] + y[m:]


def kernel(n_inst, n_axial, order, kmat, s0, f, a_hbm, c_hbm, out,
           wa, wc, sb, rb, ob, rq, u, tx, tw, inflow, outflow, inv,
           w_sem, x1_send, x1_recv, x2_send, x2_recv, pair_sem, chain_sem):
    i = lax.axis_index("inst")
    a = lax.axis_index("axial")
    local, tiles, width = s0.shape
    per = tiles // n_inst
    half = width // 2
    core = lax.rem(i, 2)
    partner = i + 1 - 2 * core
    nxt, prv = lax.rem(a + 1, n_axial), lax.rem(a + n_axial - 1, n_axial)

    load_a = pltpu.make_async_copy(a_hbm, wa, w_sem.at[0])
    load_c = pltpu.make_async_copy(c_hbm, wc, w_sem.at[1])
    load_a.start()
    load_c.start()

    barrier = pltpu.get_barrier_semaphore()
    for d in range(1, n_inst):
        pl.semaphore_signal(barrier, inc=1, device_id={"inst": lax.rem(i + d, n_inst)}, device_id_type=MESH)
    for there in (nxt, prv):
        pl.semaphore_signal(barrier, inc=1, device_id={"axial": there}, device_id_type=MESH)

    for t in range(tiles):
        sb[t, 0:local, :] = s0[:, t, :]
        sb[t, local:2 * local, :] = f[:, t, :]
    for t in range(tiles):
        pos = jnp.int32(0)
        for k in range(tiles):
            pos = jnp.where(order[k] == t, k, pos)
        inv[t] = pos
    row = lax.broadcasted_iota(jnp.int32, (half, width), 0)
    col = lax.broadcasted_iota(jnp.int32, (half, width), 1)
    tx[core, 0] = jnp.where(col == row + core * half, 1.0, 0.0).astype(F32)
    tx[core, 1] = jnp.zeros((half, width), F32)

    pl.semaphore_wait(barrier, n_inst + 1)

    def first(d):
        peer = lax.rem(i + d, n_inst)
        return pltpu.make_async_remote_copy(
            src_ref=sb.at[pl.ds(per * peer, per)], dst_ref=rb.at[i],
            send_sem=x1_send.at[d], recv_sem=x1_recv.at[d],
            device_id={"inst": peer}, device_id_type=MESH)

    def second(d):
        peer = lax.rem(i + d, n_inst)
        return pltpu.make_async_remote_copy(
            src_ref=ob.at[peer], dst_ref=rq.at[pl.ds(per * i, per)],
            send_sem=x2_send.at[d], recv_sem=x2_recv.at[d],
            device_id={"inst": peer}, device_id_type=MESH)

    for d in range(1, n_inst):
        first(d).start()
    rb[i] = sb[pl.ds(per * i, per)]

    load_a.wait()
    load_c.wait()

    def column_step(k, carry):
        t = order[k]
        c, ai = wc[t], wa[t]
        b = times(tx[core].reshape(2 * half, width), c)
        p = -times(b[:half], ai)
        tx[core, 0] = p
        tx[core, 1] = -times(p + b[half:], ai)
        return carry

    lax.fori_loop(0, tiles // 2, column_step, 0)

    for d in range(1, n_inst):
        first(d).wait_recv()
    for t in range(per):
        mixed = jnp.dot(kmat[...], rb[:, t].reshape(2 * local * n_inst, width),
                        precision=lax.Precision.HIGHEST, preferred_element_type=F32)
        ob[:, t] = mixed.reshape(n_inst, 2 * local, width)
    for d in range(1, n_inst):
        second(d).start()
    rq[pl.ds(per * i, per)] = ob[i]

    lax.fori_loop(tiles // 2, tiles, column_step, 0)

    pair = pltpu.make_async_remote_copy(
        src_ref=tx.at[core], dst_ref=tx.at[core], send_sem=pair_sem.at[0], recv_sem=pair_sem.at[1],
        device_id={"inst": partner}, device_id_type=MESH)
    pair.start()
    for d in range(1, n_inst):
        second(d).wait_recv()

    lower = lax.broadcasted_iota(jnp.int32, (2 * local, width), 0) >= local

    def data_step(k, x):
        t = order[k]
        y = times(rq[t] - times(x, wc[t]), wa[t])
        z = times(pltpu.roll(y, local, 0), wa[t])
        return jnp.where(lower, y - z, y)

    zero = jnp.zeros((2 * local, width), F32)
    shift = lax.fori_loop(0, tiles, data_step, zero)

    other = pltpu.make_async_remote_copy(
        src_ref=tx.at[1 - core], dst_ref=tx.at[1 - core], send_sem=pair_sem.at[0], recv_sem=pair_sem.at[1],
        device_id={"inst": partner}, device_id_type=MESH)
    other.wait_recv()
    pad = tw.shape[1] // 4
    for h in range(2):
        for part in range(2):
            high, low = halves(tx[h, part])
            tw[pl.ds(h * half, half), part * pad:part * pad + width] = high
            tw[pl.ds(h * half, half), (2 + part) * pad:(2 + part) * pad + width] = low

    def through(x):
        y = lax.dot_general(jnp.concatenate(halves(x), 0), tw[...], NN, preferred_element_type=F32)
        y = y[:2 * local] + y[2 * local:]
        y = y[:, :2 * pad] + y[:, 2 * pad:]
        own, cross = y[:, :width], y[:, pad:pad + width]
        return own + jnp.where(lower, pltpu.roll(cross, local, 0), 0.0)

    forward = pltpu.make_async_remote_copy(
        src_ref=outflow, dst_ref=inflow, send_sem=chain_sem.at[0], recv_sem=chain_sem.at[1],
        device_id={"axial": nxt}, device_id_type=MESH)

    @pl.when(a == 0)
    def _():
        inflow[...] = zero
        outflow[...] = shift

    @pl.when(a > 0)
    def _():
        forward.wait_recv()
        outflow[...] = through(inflow[...]) + shift

    @pl.when(a < n_axial - 1)
    def _():
        forward.start()

    def final_step(k, x):
        x = data_step(k, x)
        u[k] = x
        return x

    lax.fori_loop(0, tiles, final_step, inflow[...])
    for t in range(tiles):
        out[:, t, :] = s0[:, t, :] + u[inv[t], local:2 * local, :]

    for d in range(1, n_inst):
        first(d).wait_send()
        second(d).wait_send()
    pair.wait_send()

    @pl.when(a < n_axial - 1)
    def _():
        forward.wait_send()


def solution(mesh):
    n_inst, n_axial = mesh.shape["inst"], mesh.shape["axial"]

    def on_device(flow_state, forcing, tile_inverse, coupling, sweep_order):
        local, tiles, width = flow_state.shape
        per = tiles // n_inst
        half = width // 2
        pad = -(-width // 128) * 128
        rows = 2 * local
        kmat = jnp.asarray(exchange_matrix(local * n_inst, n_inst))
        vmem = pl.BlockSpec(memory_space=pltpu.VMEM)
        return pl.pallas_call(
            functools.partial(kernel, n_inst, n_axial),
            out_shape=jax.ShapeDtypeStruct(flow_state.shape, F32),
            in_specs=[pl.BlockSpec(memory_space=pltpu.SMEM), vmem, vmem, vmem,
                      pl.BlockSpec(memory_space=pl.ANY), pl.BlockSpec(memory_space=pl.ANY)],
            out_specs=vmem,
            scratch_shapes=[
                pltpu.VMEM((tiles, width, width), BF16),
                pltpu.VMEM((tiles, width, width), BF16),
                pltpu.VMEM((tiles, rows, width), F32),
                pltpu.VMEM((n_inst, per, rows, width), F32),
                pltpu.VMEM((n_inst, per, rows, width), F32),
                pltpu.VMEM((tiles, rows, width), F32),
                pltpu.VMEM((tiles, rows, width), F32),
                pltpu.VMEM((2, 2, half, width), F32),
                pltpu.VMEM((width, 4 * pad), BF16),
                pltpu.VMEM((rows, width), F32),
                pltpu.VMEM((rows, width), F32),
                pltpu.SMEM((tiles,), jnp.int32),
                pltpu.SemaphoreType.DMA((2,)),
                pltpu.SemaphoreType.DMA((n_inst,)),
                pltpu.SemaphoreType.DMA((n_inst,)),
                pltpu.SemaphoreType.DMA((n_inst,)),
                pltpu.SemaphoreType.DMA((n_inst,)),
                pltpu.SemaphoreType.DMA((2,)),
                pltpu.SemaphoreType.DMA((2,)),
            ],
            compiler_params=pltpu.CompilerParams(collective_id=0, has_side_effects=True),
        )(sweep_order, kmat, flow_state, forcing, tile_inverse, coupling)

    return jax.shard_map(
        on_device,
        mesh=mesh,
        in_specs=(P("inst", "axial", None), P("inst", "axial", None), P("axial", None, None),
                  P("axial", None, None), P("axial")),
        out_specs=P("inst", "axial", None),
        check_vma=False,
    )
```

time: 714 us -> 137 us (0.19)
  the two profiles are of different devices: /device:TPU:24 before, /device:TPU:250 now
where the time goes in v1:
time: 137 us
  Pallas kernels  135 us (99%)
  local copies, waits for them, and re-layouts  1.54 us (1%)
    pallas_call x1, Pallas kernels, on_device(): pl.pallas_call(functools.partial(kernel, n_inst, n_axial), out_shape=jax....  135 us

profile of v1, /device:TPU:250, one launch (start us, length us, event | category | flops | bytes accessed | tf_op | source)
XLA Modules:
  0.0 137.0 jit_solution(5476372941364654268)
XLA Ops:
  0.0 135.5 %shard_map.64 = f32[4,16,320]{2,1,0:T(8,128)} custom-call(s32[16]{0:T(128)} %order.1, f32[64,64]{1,0:T(8,128)} %constant.2.clone.kmat, f32[4,16,320]{2,1,0:T(8,128)} %s0.1, f32[4,16,320]{2,1,0:T(8,128)} %f.1, bf16[16,320,320]{2,1,0:T(8,128)(2,1)} %a_hbm.1, bf16[16,320,320]{2,1,0:T(8,128)(2,1)} %c_hbm.1), custom_call_target="tpu_custom_call" | custom-call | tf_op jit(solution)/shard_map/pallas_call | solution.py:212
  135.5 1.5 %copy.8 = f32[4,16,320]{2,1,0:T(8,128)} copy(f32[4,16,320]{2,1,0:T(8,128)} %shard_map.64) | data formatting | bytes 163840

commit v2 on v1

v2 whole, which is shorter than its diff:
```python
import functools

import jax
import jax.numpy as jnp
import numpy as np
from jax import lax
from jax.experimental import pallas as pl
from jax.experimental.pallas import tpu as pltpu
from jax.sharding import PartitionSpec as P

ITERS = 2
SPECTRAL_GAIN = 2.0
NZ = 8
CHUNK = 16
MESH = pl.DeviceIdType.MESH
F32, BF16 = jnp.float32, jnp.bfloat16
NT = (((1,), (1,)), ((), ()))
NN = (((1,), (0,)), ((), ()))


def exchange_matrix(period, groups):
    idx = np.arange(period)
    dist = idx[:, None] - idx[None, :]
    angle = np.pi * dist / period
    safe = np.where(dist == 0, 1.0, np.sin(angle))
    deriv = np.where(dist == 0, 0.0, 0.5 * (1.0 - 2.0 * (dist % 2)) * np.cos(angle) / safe)
    e = deriv * (SPECTRAL_GAIN / period) + np.eye(period)
    whole = np.block([[-e @ e, e], [-2.0 * e, 2.0 * np.eye(period)]])
    local = period // groups
    perm = np.array(
        [part * period + dev * local + n for dev in range(groups) for part in range(2) for n in range(local)]
    )
    return whole[np.ix_(perm, perm)].astype(np.float32)


def halves(x):
    high = x.astype(BF16)
    low = (x - high.astype(F32)).astype(BF16)
    return high, low


def split(x):
    high = x.astype(BF16).astype(F32)
    return jnp.concatenate([high, x - high], 0).astype(BF16)


def times(x, w, dims=NT):
    m = x.shape[0]
    y = lax.dot_general(split(x), w, dims, preferred_element_type=F32)
    return y[:m] + y[m:]


def store_map(dst, row, part, block):
    pad = dst.shape[1] // 4
    rows, width = block.shape
    high, low = halves(block)
    dst[pl.ds(row, rows), part * pad:part * pad + width] = high
    dst[pl.ds(row, rows), (2 + part) * pad:(2 + part) * pad + width] = low


def through(m, p, g):
    rows, width = p.shape
    pad = m.shape[1] // 4
    y = lax.dot_general(split(jnp.concatenate([p, g], 0)), m[...], NN, preferred_element_type=F32)
    y = y[:2 * rows] + y[2 * rows:]
    y = y[:, :2 * pad] + y[:, 2 * pad:]
    return y[:rows, :width], y[rows:, :width] + y[:rows, pad:pad + width]


def kernel(n_inst, n_axial, order, kmat, s0, f, a_hbm, c_hbm, out,
           wa, wc, sb, rb, ob, rq, u, tx, tg, tw, tp, si, so, pm, sh, uin, fwd_out, fwd_in, xin, xout, inv,
           w_sem, x1_send, x1_recv, x2_send, x2_recv, g1_send, g1_recv, sh_sem, sc_send, sc_recv,
           g2_send, g2_recv, up_send, up_recv, fw_sem, in_sem):
    i = lax.axis_index("inst")
    a = lax.axis_index("axial")
    local, tiles, width = s0.shape
    per = tiles // n_inst
    cols = width // n_inst
    chips = n_inst // 2
    x, core = i // 2, lax.rem(i, 2)
    y, z = a // NZ, lax.rem(a, NZ)
    last = n_axial // NZ - 1
    rows = si.shape[1]
    chunks = rows // CHUNK
    both = 2 * local
    hub = core == 1
    lead = (z == NZ - 1) & (y < last)

    load_a = pltpu.make_async_copy(a_hbm, wa, w_sem.at[0])
    load_c = pltpu.make_async_copy(c_hbm, wc, w_sem.at[1])
    load_a.start()
    load_c.start()

    barrier = pltpu.get_barrier_semaphore()
    for d in range(1, n_inst):
        pl.semaphore_signal(barrier, inc=1, device_id={"inst": lax.rem(i + d, n_inst)}, device_id_type=MESH)

    @pl.when(hub)
    def _():
        for d in (1, NZ - 1):
            there = y * NZ + lax.rem(z + d, NZ)
            pl.semaphore_signal(barrier, inc=1, device_id={"axial": there}, device_id_type=MESH)

        @pl.when(lead)
        def _():
            for zz in range(NZ):
                pl.semaphore_signal(barrier, inc=1, device_id={"axial": (y + 1) * NZ + zz}, device_id_type=MESH)

        @pl.when(y > 0)
        def _():
            pl.semaphore_signal(barrier, inc=1, device_id={"axial": y * NZ - 1}, device_id_type=MESH)

    for t in range(tiles):
        sb[t, 0:local, :] = s0[:, t, :]
        sb[t, local:both, :] = f[:, t, :]
    row = lax.broadcasted_iota(jnp.int32, (cols, width), 0)
    col = lax.broadcasted_iota(jnp.int32, (cols, width), 1)
    tx[0] = jnp.where(col == row + i * cols, 1.0, 0.0).astype(F32)
    tx[1] = jnp.zeros((cols, width), F32)

    pl.semaphore_wait(barrier, n_inst - 1 + jnp.where(
        hub, 2 + jnp.where(lead, NZ, 0) + jnp.where(y > 0, 1, 0), 0))

    def first(d):
        peer = lax.rem(i + d, n_inst)
        return pltpu.make_async_remote_copy(
            src_ref=sb.at[pl.ds(per * peer, per)], dst_ref=rb.at[i],
            send_sem=x1_send.at[d], recv_sem=x1_recv.at[d],
            device_id={"inst": peer}, device_id_type=MESH)

    def second(d):
        peer = lax.rem(i + d, n_inst)
        return pltpu.make_async_remote_copy(
            src_ref=ob.at[peer], dst_ref=rq.at[pl.ds(per * i, per)],
            send_sem=x2_send.at[d], recv_sem=x2_recv.at[d],
            device_id={"inst": peer}, device_id_type=MESH)

    for d in range(1, n_inst):
        first(d).start()
    rb[i] = sb[pl.ds(per * i, per)]
    for t in range(tiles):
        pos = jnp.int32(0)
        for k in range(tiles):
            pos = jnp.where(order[k] == t, k, pos)
        inv[t] = pos

    load_a.wait()
    load_c.wait()

    def column_step(k, carry):
        t = order[k]
        c, ai = wc[t], wa[t]
        b = times(tx[...].reshape(2 * cols, width), c)
        p = -times(b[:cols], ai)
        tx[0] = p
        tx[1] = -times(p + b[cols:], ai)
        return carry

    lax.fori_loop(0, tiles // 2, column_step, 0)

    for d in range(1, n_inst):
        first(d).wait_recv()
    for t in range(per):
        mixed = jnp.dot(kmat[...], rb[:, t].reshape(both * n_inst, width),
                        precision=lax.Precision.HIGHEST, preferred_element_type=F32)
        ob[:, t] = mixed.reshape(n_inst, both, width)
    for d in range(1, n_inst):
        second(d).start()
    rq[pl.ds(per * i, per)] = ob[i]

    lax.fori_loop(tiles // 2, tiles, column_step, 0)

    def gather(xx, sender):
        return pltpu.make_async_remote_copy(
            src_ref=tx, dst_ref=tg.at[sender // 2, :, pl.ds(pl.multiple_of(lax.rem(sender, 2) * cols, 8), cols)],
            send_sem=g1_send.at[xx], recv_sem=g1_recv.at[sender],
            device_id={"inst": 2 * xx + 1}, device_id_type=MESH)

    for xx in range(chips):
        @pl.when(2 * xx + 1 != i)
        def _(xx=xx):
            gather(xx, i).start()

    for d in range(1, n_inst):
        second(d).wait_recv()

    lower = lax.broadcasted_iota(jnp.int32, (both, width), 0) >= local

    def data_step(k, v):
        t = order[k]
        r = times(rq[t] - times(v, wc[t]), wa[t])
        q = times(pltpu.roll(r, local, 0), wa[t])
        return jnp.where(lower, r - q, r)

    zero = jnp.zeros((both, width), F32)
    shift = lax.fori_loop(0, tiles, data_step, zero)

    share = pltpu.make_async_remote_copy(
        src_ref=sh.at[0], dst_ref=sh.at[1], send_sem=sh_sem.at[0], recv_sem=sh_sem.at[1],
        device_id={"inst": lax.rem(i + 1, n_inst)}, device_id_type=MESH)
    give = pltpu.make_async_remote_copy(
        src_ref=xout, dst_ref=xin, send_sem=in_sem.at[0], recv_sem=in_sem.at[1],
        device_id={"inst": lax.rem(i + n_inst - 1, n_inst)}, device_id_type=MESH)

    @pl.when(core == 0)
    def _():
        sh[0] = shift
        share.start()
        share.wait_send()
        give.wait_recv()

    @pl.when(hub)
    def _():
        tg[x, :, pl.ds(cols, cols)] = tx[...]
        for j in range(n_inst):
            @pl.when(j != i)
            def _(j=j):
                gather(0, j).wait_recv()
        for xx in range(chips):
            for part in range(2):
                store_map(tw, 2 * cols * xx, part, tg[xx, part])
        share.wait_recv()
        other = sh[1]
        bp = jnp.where(lower, pltpu.roll(shift, local, 0), other)
        bg = jnp.where(lower, shift, pltpu.roll(other, local, 0))

        def scan(c):
            part = pl.ds(pl.multiple_of(c * CHUNK, CHUNK), CHUNK)
            return pltpu.make_async_remote_copy(
                src_ref=so.at[:, part], dst_ref=si.at[:, part],
                send_sem=sc_send.at[c], recv_sem=sc_recv.at[c],
                device_id={"axial": y * NZ + lax.rem(z + 1, NZ)}, device_id_type=MESH)

        def spread(src, c, d):
            part = pl.ds(pl.multiple_of(c * CHUNK, CHUNK), CHUNK)
            return pltpu.make_async_remote_copy(
                src_ref=src.at[:, part], dst_ref=pm.at[x, :, part],
                send_sem=g2_send.at[d - 1, c], recv_sem=g2_recv.at[d - 1, c],
                device_id={"inst": lax.rem(i + 2 * d, n_inst)}, device_id_type=MESH)

        def down(zz):
            return pltpu.make_async_remote_copy(
                src_ref=uin.at[0], dst_ref=uin.at[1], send_sem=up_send.at[zz], recv_sem=up_recv.at[0],
                device_id={"axial": lax.rem(y + 1, last + 1) * NZ + zz}, device_id_type=MESH)

        hop = pltpu.make_async_remote_copy(
            src_ref=fwd_out, dst_ref=fwd_in, send_sem=fw_sem.at[0], recv_sem=fw_sem.at[1],
            device_id={"axial": y * NZ + lax.rem(z + 1, NZ)}, device_id_type=MESH)

        count = jnp.where(y == 0, 1, chunks)
        mapped = (y > 0) & (z > 0)

        @pl.when(z == 0)
        def _():
            so[0, 0:both] = bp
            so[1, 0:both] = bg
            so[:, both:both + 2 * cols] = tg[x]
            so[:, both + 2 * cols:] = jnp.zeros((2, rows - both - 2 * cols, width), F32)
            lax.fori_loop(0, count, lambda c, k: (scan(c).start(), k)[1], 0)

        @pl.when(z > 0)
        def _():
            empty = jnp.zeros((CHUNK - both, width), F32)
            add_p = jnp.concatenate([bp, empty], 0)
            add_g = jnp.concatenate([bg, empty], 0)

            def chunk_step(c, carry):
                scan(c).wait_recv()
                part = pl.ds(pl.multiple_of(c * CHUNK, CHUNK), CHUNK)

                @pl.when(mapped & jnp.logical_not(lead))
                def _():
                    for d in range(1, chips):
                        spread(si, c, d).start()

                p, g = through(tw, si[0, part], si[1, part])
                so[0, part] = p + jnp.where(c == 0, add_p, 0.0)
                so[1, part] = g + jnp.where(c == 0, add_g, 0.0)

                @pl.when(z < NZ - 1)
                def _():
                    scan(c).start()

                @pl.when(mapped & lead)
                def _():
                    for d in range(1, chips):
                        spread(so, c, d).start()
                return carry

            lax.fori_loop(0, count, chunk_step, 0)

        @pl.when(mapped)
        def _():
            @pl.when(lead)
            def _():
                pm[x] = so[...]

            @pl.when(jnp.logical_not(lead))
            def _():
                pm[x] = si[...]

            for d in range(1, chips):
                for c in range(chunks):
                    spread(si, c, d).wait_recv()
            for xx in range(chips):
                for part in range(2):
                    store_map(tp, 2 * cols * xx, part, pm[xx, part, both:both + 2 * cols])

        @pl.when((y == 0) & (z == NZ - 1))
        def _():
            uin[0] = so[:, 0:both]
            for zz in range(NZ):
                down(zz).start()

        @pl.when(y > 0)
        def _():
            down(0).wait_recv()

        def give_out(p, g):
            xout[...] = jnp.where(lower, pltpu.roll(g, local, 0), p)
            give.start()
            xin[...] = jnp.where(lower, g, pltpu.roll(p, local, 0))

        @pl.when(mapped)
        def _():
            p, g = through(tp, uin[1, 0], uin[1, 1])

            @pl.when(lead)
            def _():
                uin[0, 0] = p + so[0, 0:both]
                uin[0, 1] = g + so[1, 0:both]
                for zz in range(NZ):
                    down(zz).start()
                hop.wait_recv()
                give_out(fwd_in[0], fwd_in[1])

            @pl.when(jnp.logical_not(lead))
            def _():
                here_p, here_g = p + si[0, 0:both], g + si[1, 0:both]
                give_out(here_p, here_g)

                @pl.when((z == NZ - 2) & (y < last))
                def _():
                    next_p, next_g = through(tw, here_p, here_g)
                    fwd_out[0] = next_p + bp
                    fwd_out[1] = next_g + bg
                    hop.start()

        @pl.when((y > 0) & (z == 0))
        def _():
            give_out(uin[1, 0], uin[1, 1])

        @pl.when((y == 0) & (z == 0))
        def _():
            give_out(zero, zero)

        @pl.when((y == 0) & (z > 0))
        def _():
            give_out(si[0, 0:both], si[1, 0:both])

    def final_step(k, v):
        v = data_step(k, v)
        u[k] = v
        return v

    lax.fori_loop(0, tiles, final_step, xin[...])
    for t in range(tiles):
        out[:, t, :] = s0[:, t, :] + u[inv[t], local:both, :]

    for d in range(1, n_inst):
        first(d).wait_send()
        second(d).wait_send()
    for xx in range(chips):
        @pl.when(2 * xx + 1 != i)
        def _(xx=xx):
            gather(xx, i).wait_send()

    @pl.when(hub)
    def _():
        give.wait_send()
        count = jnp.where(y == 0, 1, chunks)

        @pl.when(z < NZ - 1)
        def _():
            lax.fori_loop(0, count, lambda c, k: (pltpu.make_async_remote_copy(
                src_ref=so.at[:, pl.ds(0, CHUNK)], dst_ref=si.at[:, pl.ds(0, CHUNK)],
                send_sem=sc_send.at[c], recv_sem=sc_recv.at[c],
                device_id={"axial": y * NZ + lax.rem(z + 1, NZ)}, device_id_type=MESH).wait_send(), k)[1], 0)

        @pl.when((y > 0) & (z > 0))
        def _():
            for d in range(1, chips):
                for c in range(chunks):
                    pltpu.make_async_remote_copy(
                        src_ref=si.at[:, pl.ds(0, CHUNK)], dst_ref=pm.at[x, :, pl.ds(0, CHUNK)],
                        send_sem=g2_send.at[d - 1, c], recv_sem=g2_recv.at[d - 1, c],
                        device_id={"inst": lax.rem(i + 2 * d, n_inst)}, device_id_type=MESH).wait_send()

        @pl.when(lead)
        def _():
            for zz in range(NZ):
                pltpu.make_async_remote_copy(
                    src_ref=uin.at[0], dst_ref=uin.at[1], send_sem=up_send.at[zz], recv_sem=up_recv.at[0],
                    device_id={"axial": lax.rem(y + 1, last + 1) * NZ + zz}, device_id_type=MESH).wait_send()

        @pl.when((y > 0) & (z == NZ - 2) & (y < last))
        def _():
            pltpu.make_async_remote_copy(
                src_ref=fwd_out, dst_ref=fwd_in, send_sem=fw_sem.at[0], recv_sem=fw_sem.at[1],
                device_id={"axial": y * NZ + lax.rem(z + 1, NZ)}, device_id_type=MESH).wait_send()


def solution(mesh):
    n_inst, n_axial = mesh.shape["inst"], mesh.shape["axial"]

    def on_device(flow_state, forcing, tile_inverse, coupling, sweep_order):
        local, tiles, width = flow_state.shape
        per = tiles // n_inst
        cols = width // n_inst
        chips = n_inst // 2
        pad = -(-width // 128) * 128
        both = 2 * local
        rows = -(-(both + 2 * cols) // CHUNK) * CHUNK
        chunks = rows // CHUNK
        kmat = jnp.asarray(exchange_matrix(local * n_inst, n_inst))
        vmem = pl.BlockSpec(memory_space=pltpu.VMEM)
        dma = pltpu.SemaphoreType.DMA
        return pl.pallas_call(
            functools.partial(kernel, n_inst, n_axial),
            out_shape=jax.ShapeDtypeStruct(flow_state.shape, F32),
            in_specs=[pl.BlockSpec(memory_space=pltpu.SMEM), vmem, vmem, vmem,
                      pl.BlockSpec(memory_space=pl.ANY), pl.BlockSpec(memory_space=pl.ANY)],
            out_specs=vmem,
            scratch_shapes=[
                pltpu.VMEM((tiles, width, width), BF16),
                pltpu.VMEM((tiles, width, width), BF16),
                pltpu.VMEM((tiles, both, width), F32),
                pltpu.VMEM((n_inst, per, both, width), F32),
                pltpu.VMEM((n_inst, per, both, width), F32),
                pltpu.VMEM((tiles, both, width), F32),
                pltpu.VMEM((tiles, both, width), F32),
                pltpu.VMEM((2, cols, width), F32),
                pltpu.VMEM((chips, 2, 2 * cols, width), F32),
                pltpu.VMEM((width, 4 * pad), BF16),
                pltpu.VMEM((width, 4 * pad), BF16),
                pltpu.VMEM((2, rows, width), F32),
                pltpu.VMEM((2, rows, width), F32),
                pltpu.VMEM((chips, 2, rows, width), F32),
                pltpu.VMEM((2, both, width), F32),
                pltpu.VMEM((2, 2, both, width), F32),
                pltpu.VMEM((2, both, width), F32),
                pltpu.VMEM((2, both, width), F32),
                pltpu.VMEM((both, width), F32),
                pltpu.VMEM((both, width), F32),
                pltpu.SMEM((tiles,), jnp.int32),
                dma((2,)),
                dma((n_inst,)), dma((n_inst,)), dma((n_inst,)), dma((n_inst,)),
                dma((chips,)), dma((n_inst,)),
                dma((2,)),
                dma((chunks,)), dma((chunks,)),
                dma((chips - 1, chunks)), dma((chips - 1, chunks)),
                dma((NZ,)), dma((1,)),
                dma((2,)), dma((2,)),
            ],
            compiler_params=pltpu.CompilerParams(collective_id=0, has_side_effects=True),
        )(sweep_order, kmat, flow_state, forcing, tile_inverse, coupling)

    return jax.shard_map(
        on_device,
        mesh=mesh,
        in_specs=(P("inst", "axial", None), P("inst", "axial", None), P("axial", None, None),
                  P("axial", None, None), P("axial")),
        out_specs=P("inst", "axial", None),
        check_vma=False,
    )
```

time: 137 us -> 70.2 us (0.51)
  the two profiles are of different devices: /device:TPU:250 before, /device:TPU:24 now
where the time goes in v2:
time: 70.2 us; the launch traced here: 70 us
  Pallas kernels  68.4 us (97%)
  local copies, waits for them, and re-layouts  1.54 us (2%)
    pallas_call x1, Pallas kernels, on_device(): pl.pallas_call(functools.partial(kernel, n_inst, n_axial), out_shape=jax....  68.4 us
    unnamed x1, local copies, waits for them, and re-layouts  1.54 us

profile of v2, /device:TPU:24, one launch (start us, length us, event | category | flops | bytes accessed | tf_op | source)
XLA Modules:
  0.0 70.0 jit_solution(5685743702148788139)
XLA Ops:
  0.0 68.4 %shard_map.64 = f32[4,16,320]{2,1,0:T(8,128)} custom-call(s32[16]{0:T(128)} %order.1, f32[64,64]{1,0:T(8,128)} %constant.2.clone.kmat, f32[4,16,320]{2,1,0:T(8,128)} %s0.1, f32[4,16,320]{2,1,0:T(8,128)} %f.1, bf16[16,320,320]{2,1,0:T(8,128)(2,1)} %a_hbm.1, bf16[16,320,320]{2,1,0:T(8,128)(2,1)} %c_hbm.1), custom_call_target="tpu_custom_call" | custom-call | tf_op jit(solution)/shard_map/pallas_call | solution.py:428
  68.4 1.5 %copy.8 = f32[4,16,320]{2,1,0:T(8,128)} copy(f32[4,16,320]{2,1,0:T(8,128)} %shard_map.64) | data formatting | bytes 163840

commit v3 on v2

v3 whole, which is shorter than its diff:
```python
import functools

import jax
import jax.numpy as jnp
import numpy as np
from jax import lax
from jax.experimental import pallas as pl
from jax.experimental.pallas import tpu as pltpu
from jax.sharding import PartitionSpec as P

ITERS = 2
SPECTRAL_GAIN = 2.0
NZ = 8
MIX_AT = 12
CHUNK = 16
MESH = pl.DeviceIdType.MESH
F32, BF16 = jnp.float32, jnp.bfloat16
NT = (((1,), (1,)), ((), ()))
NN = (((1,), (0,)), ((), ()))


def exchange_matrix(period, groups):
    idx = np.arange(period)
    dist = idx[:, None] - idx[None, :]
    angle = np.pi * dist / period
    safe = np.where(dist == 0, 1.0, np.sin(angle))
    deriv = np.where(dist == 0, 0.0, 0.5 * (1.0 - 2.0 * (dist % 2)) * np.cos(angle) / safe)
    e = deriv * (SPECTRAL_GAIN / period) + np.eye(period)
    whole = np.block([[-e @ e, e], [-2.0 * e, 2.0 * np.eye(period)]])
    local = period // groups
    given = [part * period + dev * local + n for dev in range(groups) for part in range(2) for n in range(local)]
    wide = 2 * local
    made = [part * period + chip * wide + n for chip in range(groups // 2) for part in range(2) for n in range(wide)]
    return whole[np.ix_(made, given)].astype(np.float32)


def halves(x):
    high = x.astype(BF16)
    low = (x - high.astype(F32)).astype(BF16)
    return high, low


def split(x):
    high = x.astype(BF16).astype(F32)
    return jnp.concatenate([high, x - high], 0).astype(BF16)


def times(x, w, dims=NT):
    m = x.shape[0]
    y = lax.dot_general(split(x), w, dims, preferred_element_type=F32)
    return y[:m] + y[m:]


def store_map(dst, row, part, block):
    pad = dst.shape[1] // 4
    rows, width = block.shape
    high, low = halves(block)
    dst[pl.ds(row, rows), part * pad:part * pad + width] = high
    dst[pl.ds(row, rows), (2 + part) * pad:(2 + part) * pad + width] = low


def through(m, p, g):
    rows, width = p.shape
    pad = m.shape[1] // 4
    y = lax.dot_general(split(jnp.concatenate([p, g], 0)), m[...], NN, preferred_element_type=F32)
    y = y[:2 * rows] + y[2 * rows:]
    y = y[:, :2 * pad] + y[:, 2 * pad:]
    return y[:rows, :width], y[rows:, :width] + y[:rows, pad:pad + width]


def kernel(n_inst, n_axial, order, kmat, s0, f, a_hbm, c_hbm, out,
           wa, wc, sb, rb, ob, rq, u, tx, txm, tg, tgm, tw, tp, si, so, pm, sh, uin, fwd, vin, inv,
           w_sem, x1_send, x1_recv, x2_send, x2_recv, g1_send, g1_recv, gm_send, gm_recv, pair_sem,
           sc_send, sc_recv, sd_sem, g2_send, g2_recv, up_send, up_recv, fw_sem):
    i = lax.axis_index("inst")
    a = lax.axis_index("axial")
    local, tiles, width = s0.shape
    chips = n_inst // 2
    per = tiles // chips
    mid = tiles // 2
    cols = width // n_inst
    block = 2 * cols
    both = 2 * local
    x, core = i // 2, lax.rem(i, 2)
    y, z = a // NZ, lax.rem(a, NZ)
    last = n_axial // NZ - 1
    chunks = block // CHUNK
    hub = core == 1
    lead = (z == NZ - 1) & (y < last)
    mapped = (y > 0) & (z > 0)
    data = pl.ds(block, both)

    load_a = pltpu.make_async_copy(a_hbm, wa, w_sem.at[0])
    load_c = pltpu.make_async_copy(c_hbm, wc, w_sem.at[1])
    load_a.start()
    load_c.start()

    def remote(src, dst, send, recv, **there):
        return pltpu.make_async_remote_copy(
            src_ref=src, dst_ref=dst, send_sem=send, recv_sem=recv, device_id=there, device_id_type=MESH)

    barrier = pltpu.get_barrier_semaphore()
    for d in range(1, n_inst):
        pl.semaphore_signal(barrier, inc=1, device_id={"inst": lax.rem(i + d, n_inst)}, device_id_type=MESH)

    @pl.when(hub)
    def _():
        for d in (1, NZ - 1):
            there = y * NZ + lax.rem(z + d, NZ)
            pl.semaphore_signal(barrier, inc=1, device_id={"axial": there}, device_id_type=MESH)

        @pl.when(lead)
        def _():
            for zz in range(NZ):
                pl.semaphore_signal(barrier, inc=1, device_id={"axial": (y + 1) * NZ + zz}, device_id_type=MESH)

        @pl.when(y > 0)
        def _():
            pl.semaphore_signal(barrier, inc=1, device_id={"axial": y * NZ - 1}, device_id_type=MESH)

    for t in range(tiles):
        sb[t, 0:local, :] = s0[:, t, :]
        sb[t, local:both, :] = f[:, t, :]
    row = lax.broadcasted_iota(jnp.int32, (cols, width), 0)
    col = lax.broadcasted_iota(jnp.int32, (cols, width), 1)
    tx[0] = jnp.where(col == row + i * cols, 1.0, 0.0).astype(F32)
    tx[1] = jnp.zeros((cols, width), F32)

    pl.semaphore_wait(barrier, n_inst - 1 + jnp.where(
        hub, 2 + jnp.where(lead, NZ, 0) + jnp.where(y > 0, 1, 0), 0))

    def first(xx, sender):
        return remote(sb.at[pl.ds(per * xx, per)], rb.at[sender], x1_send.at[xx], x1_recv.at[sender], inst=2 * xx)

    def second(d):
        xx = lax.rem(x + d, chips)
        return remote(ob.at[xx], rq.at[pl.ds(per * x, per)], x2_send.at[d], x2_recv.at[d], inst=2 * xx)

    def gather(src, dst, send, recv, xx, sender):
        half = pl.ds(pl.multiple_of(lax.rem(sender, 2) * cols, 8), cols)
        return remote(src, dst.at[sender // 2, :, half], send.at[xx], recv.at[sender], inst=2 * xx + 1)

    def whole(xx, sender):
        return gather(tx, tg, g1_send, g1_recv, xx, sender)

    def halfway(xx, sender):
        return gather(txm, tgm, gm_send, gm_recv, xx, sender)

    def to_hubs(copy):
        for xx in range(chips):
            @pl.when(2 * xx + 1 != i)
            def _(xx=xx):
                copy(xx, i).start()

    other = i + 1 - 2 * core
    pass_rq = remote(rq, rq, pair_sem.at[0], pair_sem.at[1], inst=other)
    share = remote(sh.at[0], sh.at[1], pair_sem.at[2], pair_sem.at[3], inst=other)
    give = remote(vin.at[0], vin.at[1], pair_sem.at[4], pair_sem.at[5], inst=other)
    early = remote(u.at[pl.ds(0, mid)], u.at[pl.ds(0, mid)], pair_sem.at[6], pair_sem.at[7], inst=other)
    late = remote(u.at[pl.ds(mid, mid)], u.at[pl.ds(mid, mid)], pair_sem.at[8], pair_sem.at[9], inst=other)

    for xx in range(chips):
        @pl.when(2 * xx != i)
        def _(xx=xx):
            first(xx, i).start()
    for t in range(tiles):
        pos = jnp.int32(0)
        for k in range(tiles):
            pos = jnp.where(order[k] == t, k, pos)
        inv[t] = pos

    load_a.wait()
    load_c.wait()

    def column_step(k, carry):
        t = order[k]
        c, ai = wc[t], wa[t]
        b = times(tx[...].reshape(block, width), c)
        p = -times(b[:cols], ai)
        tx[0] = p
        tx[1] = -times(p + b[cols:], ai)
        return carry

    lax.fori_loop(0, mid, column_step, 0)
    txm[...] = tx[...]
    lax.fori_loop(mid, MIX_AT, column_step, 0)

    @pl.when(core == 0)
    def _():
        rb[i] = sb[pl.ds(per * x, per)]
        for j in range(n_inst):
            @pl.when(j != i)
            def _(j=j):
                first(0, j).wait_recv()
        for t in range(per):
            mixed = jnp.dot(kmat[...], rb[:, t].reshape(both * n_inst, width),
                            precision=lax.Precision.HIGHEST, preferred_element_type=F32)
            ob[:, t] = mixed.reshape(chips, 2 * both, width)
        for d in range(1, chips):
            second(d).start()
        rq[pl.ds(per * x, per)] = ob[x]

    lax.fori_loop(MIX_AT, tiles, column_step, 0)
    to_hubs(whole)

    def data_step(k, v):
        t = order[k]
        r = times(rq[t] - times(v, wc[t]), wa[t])
        q = times(r[:both], wa[t])
        return jnp.concatenate([r[:both], r[both:] - q], 0)

    def final_step(k, v):
        v = data_step(k, v)
        u[k] = v[both:]
        return v

    zero = jnp.zeros((both, width), F32)

    @pl.when(core == 0)
    def _():
        for d in range(1, chips):
            second(d).wait_recv()
        pass_rq.start()
        v = lax.fori_loop(0, mid, data_step, jnp.zeros((2 * both, width), F32))
        sh[0, 0] = v
        sh[0, 1] = lax.fori_loop(mid, tiles, data_step, v)
        share.start()
        to_hubs(halfway)
        give.wait_recv()
        lax.fori_loop(0, mid, final_step, vin[1])
        early.start()
        late.wait_recv()
        for t in range(tiles):
            out[:, t, :] = s0[:, t, :] + u[inv[t], 0:local, :]
        early.wait_send()
        share.wait_send()
        pass_rq.wait_send()
        for d in range(1, chips):
            second(d).wait_send()

    @pl.when(hub)
    def _():
        def scan(c):
            part = pl.ds(pl.multiple_of(c * CHUNK, CHUNK), CHUNK)
            return remote(so.at[:, part], si.at[:, part], sc_send.at[c], sc_recv.at[c],
                          axial=y * NZ + lax.rem(z + 1, NZ))

        scan_data = remote(so.at[:, data], si.at[:, data], sd_sem.at[0], sd_sem.at[1],
                           axial=y * NZ + lax.rem(z + 1, NZ))

        def spread(src, c, d):
            part = pl.ds(pl.multiple_of(c * CHUNK, CHUNK), CHUNK)
            return remote(src.at[:, part], pm.at[x, :, part], g2_send.at[d - 1, c], g2_recv.at[d - 1, c],
                          inst=lax.rem(i + 2 * d, n_inst))

        def down(zz):
            return remote(uin.at[0], uin.at[1], up_send.at[zz], up_recv.at[0],
                          axial=lax.rem(y + 1, last + 1) * NZ + zz)

        hop = remote(fwd.at[0], fwd.at[1], fw_sem.at[0], fw_sem.at[1], axial=y * NZ + lax.rem(z + 1, NZ))
        count = jnp.where(y == 0, 0, chunks)

        tg[x, :, pl.ds(cols, cols)] = tx[...]
        tgm[x, :, pl.ds(cols, cols)] = txm[...]
        whole(0, i - 1).wait_recv()

        @pl.when((z == 0) & (y > 0))
        def _():
            so[:, 0:block] = tg[x]
            lax.fori_loop(0, count, lambda c, k: (scan(c).start(), k)[1], 0)

        for j in range(n_inst):
            @pl.when((j != i) & (j != i - 1))
            def _(j=j):
                whole(0, j).wait_recv()

        @pl.when(z > 0)
        def _():
            for xx in range(chips):
                for part in range(2):
                    store_map(tw, block * xx, part, tg[xx, part])

        to_hubs(halfway)

        @pl.when(z > 0)
        def _():
            def chunk_step(c, carry):
                scan(c).wait_recv()
                part = pl.ds(pl.multiple_of(c * CHUNK, CHUNK), CHUNK)

                @pl.when(jnp.logical_not(lead))
                def _():
                    for d in range(1, chips):
                        spread(si, c, d).start()

                @pl.when((y < last) | (z < NZ - 1))
                def _():
                    p, g = through(tw, si[0, part], si[1, part])
                    so[0, part] = p
                    so[1, part] = g

                @pl.when(z < NZ - 1)
                def _():
                    scan(c).start()

                @pl.when(lead)
                def _():
                    for d in range(1, chips):
                        spread(so, c, d).start()
                return carry

            lax.fori_loop(0, count, chunk_step, 0)

        share.wait_recv()
        bp, bg = sh[1, 1, 0:both], sh[1, 1, both:]

        @pl.when(z == 0)
        def _():
            so[0, data] = bp
            so[1, data] = bg
            scan_data.start()

        @pl.when(z > 0)
        def _():
            scan_data.wait_recv()

            @pl.when((y < last) | (z < NZ - 1))
            def _():
                p, g = through(tw, si[0, data], si[1, data])
                so[0, data] = p + bp
                so[1, data] = g + bg

            @pl.when(z < NZ - 1)
            def _():
                scan_data.start()

        @pl.when((y == 0) & (z == NZ - 1))
        def _():
            uin[0] = so[:, data]
            for zz in range(NZ):
                down(zz).start()

        @pl.when(mapped)
        def _():
            @pl.when(lead)
            def _():
                pm[x] = so[:, 0:block]

            @pl.when(jnp.logical_not(lead))
            def _():
                pm[x] = si[:, 0:block]

            for d in range(1, chips):
                for c in range(chunks):
                    spread(si, c, d).wait_recv()
            for xx in range(chips):
                for part in range(2):
                    store_map(tp, block * xx, part, pm[xx, part])

        def give_out(p, g):
            vin[0, 0:both] = p
            vin[0, both:] = g
            give.start()

        @pl.when(y == 0)
        def _():
            @pl.when(z == 0)
            def _():
                give_out(zero, zero)

            @pl.when(z > 0)
            def _():
                give_out(si[0, data], si[1, data])

        for j in range(n_inst):
            @pl.when(j != i)
            def _(j=j):
                halfway(0, j).wait_recv()

        def middle_map():
            for xx in range(chips):
                for part in range(2):
                    store_map(tw, block * xx, part, tgm[xx, part])

        @pl.when((y == 0) | (z != NZ - 2) | (y == last))
        def _():
            middle_map()

        @pl.when(y > 0)
        def _():
            down(0).wait_recv()

        @pl.when(mapped)
        def _():
            p, g = through(tp, uin[1, 0], uin[1, 1])

            @pl.when(lead)
            def _():
                uin[0, 0] = p + so[0, data]
                uin[0, 1] = g + so[1, data]
                for zz in range(NZ):
                    down(zz).start()
                hop.wait_recv()
                give_out(fwd[1, 0], fwd[1, 1])

            @pl.when(jnp.logical_not(lead))
            def _():
                here_p, here_g = p + si[0, data], g + si[1, data]
                give_out(here_p, here_g)

                @pl.when((z == NZ - 2) & (y < last))
                def _():
                    next_p, next_g = through(tw, here_p, here_g)
                    fwd[0, 0] = next_p + bp
                    fwd[0, 1] = next_g + bg
                    hop.start()
                    middle_map()

        @pl.when((y > 0) & (z == 0))
        def _():
            give_out(uin[1, 0], uin[1, 1])

        p, g = through(tw, vin[0, 0:both], vin[0, both:])
        pass_rq.wait_recv()
        lax.fori_loop(mid, tiles, final_step, jnp.concatenate([p, g], 0) + sh[1, 0])
        late.start()
        early.wait_recv()
        for t in range(tiles):
            out[:, t, :] = s0[:, t, :] + u[inv[t], local:both, :]

        late.wait_send()
        give.wait_send()

        @pl.when(z < NZ - 1)
        def _():
            scan_data.wait_send()
            lax.fori_loop(0, count, lambda c, k: (scan(c).wait_send(), k)[1], 0)

        @pl.when(mapped)
        def _():
            for d in range(1, chips):
                for c in range(chunks):
                    spread(si, c, d).wait_send()

        @pl.when(lead)
        def _():
            for zz in range(NZ):
                down(zz).wait_send()

        @pl.when((y > 0) & (z == NZ - 2) & (y < last))
        def _():
            hop.wait_send()

    for xx in range(chips):
        @pl.when(2 * xx != i)
        def _(xx=xx):
            first(xx, i).wait_send()

        @pl.when(2 * xx + 1 != i)
        def _(xx=xx):
            whole(xx, i).wait_send()
            halfway(xx, i).wait_send()


def solution(mesh):
    n_inst, n_axial = mesh.shape["inst"], mesh.shape["axial"]

    def on_device(flow_state, forcing, tile_inverse, coupling, sweep_order):
        local, tiles, width = flow_state.shape
        chips = n_inst // 2
        per = tiles // chips
        cols = width // n_inst
        block = 2 * cols
        pad = -(-width // 128) * 128
        both = 2 * local
        chunks = block // CHUNK
        kmat = jnp.asarray(exchange_matrix(local * n_inst, n_inst))
        vmem = pl.BlockSpec(memory_space=pltpu.VMEM)
        dma = pltpu.SemaphoreType.DMA
        return pl.pallas_call(
            functools.partial(kernel, n_inst, n_axial),
            out_shape=jax.ShapeDtypeStruct(flow_state.shape, F32),
            in_specs=[pl.BlockSpec(memory_space=pltpu.SMEM), vmem, vmem, vmem,
                      pl.BlockSpec(memory_space=pl.ANY), pl.BlockSpec(memory_space=pl.ANY)],
            out_specs=vmem,
            scratch_shapes=[
                pltpu.VMEM((tiles, width, width), BF16),
                pltpu.VMEM((tiles, width, width), BF16),
                pltpu.VMEM((tiles, both, width), F32),
                pltpu.VMEM((n_inst, per, both, width), F32),
                pltpu.VMEM((chips, per, 2 * both, width), F32),
                pltpu.VMEM((tiles, 2 * both, width), F32),
                pltpu.VMEM((tiles, both, width), F32),
                pltpu.VMEM((2, cols, width), F32),
                pltpu.VMEM((2, cols, width), F32),
                pltpu.VMEM((chips, 2, block, width), F32),
                pltpu.VMEM((chips, 2, block, width), F32),
                pltpu.VMEM((width, 4 * pad), BF16),
                pltpu.VMEM((width, 4 * pad), BF16),
                pltpu.VMEM((2, block + both, width), F32),
                pltpu.VMEM((2, block + both, width), F32),
                pltpu.VMEM((chips, 2, block, width), F32),
                pltpu.VMEM((2, 2, 2 * both, width), F32),
                pltpu.VMEM((2, 2, both, width), F32),
                pltpu.VMEM((2, 2, both, width), F32),
                pltpu.VMEM((2, 2 * both, width), F32),
                pltpu.SMEM((tiles,), jnp.int32),
                dma((2,)),
                dma((chips,)), dma((n_inst,)), dma((chips,)), dma((chips,)),
                dma((chips,)), dma((n_inst,)), dma((chips,)), dma((n_inst,)),
                dma((10,)),
                dma((chunks,)), dma((chunks,)), dma((2,)),
                dma((chips - 1, chunks)), dma((chips - 1, chunks)),
                dma((NZ,)), dma((1,)),
                dma((2,)),
            ],
            compiler_params=pltpu.CompilerParams(collective_id=0, has_side_effects=True),
        )(sweep_order, kmat, flow_state, forcing, tile_inverse, coupling)

    return jax.shard_map(
        on_device,
        mesh=mesh,
        in_specs=(P("inst", "axial", None), P("inst", "axial", None), P("axial", None, None),
                  P("axial", None, None), P("axial")),
        out_specs=P("inst", "axial", None),
        check_vma=False,
    )
```

time: 70.2 us -> 63.4 us (0.903)
  Pallas kernels: 68.4 us -> 60.9 us
    pallas_call x1, Pallas kernels: 68.4 us -> 60.9 us  [on_device(): pl.pallas_call(functools.partial(kernel, n_inst, n_axial), out_shape=jax....]
where the time goes in v3:
time: 63.4 us; the launch traced here: 62.5 us
  Pallas kernels  60.9 us (96%)
  local copies, waits for them, and re-layouts  1.54 us (2%)
    pallas_call x1, Pallas kernels, on_device(): pl.pallas_call(functools.partial(kernel, n_inst, n_axial), out_shape=jax....  60.9 us
    unnamed x1, local copies, waits for them, and re-layouts  1.54 us

profile of v3, /device:TPU:24, one launch (start us, length us, event | category | flops | bytes accessed | tf_op | source)
XLA Modules:
  0.0 62.5 jit_solution(17799031134380880965)
XLA Ops:
  0.0 60.9 %shard_map.64 = f32[4,16,320]{2,1,0:T(8,128)} custom-call(s32[16]{0:T(128)} %order.1, f32[64,64]{1,0:T(8,128)} %constant.2.clone.kmat, f32[4,16,320]{2,1,0:T(8,128)} %s0.1, f32[4,16,320]{2,1,0:T(8,128)} %f.1, bf16[16,320,320]{2,1,0:T(8,128)(2,1)} %a_hbm.1, bf16[16,320,320]{2,1,0:T(8,128)(2,1)} %c_hbm.1), custom_call_target="tpu_custom_call" | custom-call | tf_op jit(solution)/shard_map/pallas_call | solution.py:480
  60.9 1.5 %copy.8 = f32[4,16,320]{2,1,0:T(8,128)} copy(f32[4,16,320]{2,1,0:T(8,128)} %shard_map.64) | data formatting | bytes 163840

commit v4 on v3

--- a/solution.py
+++ b/solution.py
@@ -11,7 +11,7 @@
 ITERS = 2
 SPECTRAL_GAIN = 2.0
 NZ = 8
-MIX_AT = 12
+UNROLL = 4
 CHUNK = 16
 MESH = pl.DeviceIdType.MESH
 F32, BF16 = jnp.float32, jnp.bfloat16
@@ -69,9 +69,9 @@
 
 
 def kernel(n_inst, n_axial, order, kmat, s0, f, a_hbm, c_hbm, out,
-           wa, wc, sb, rb, ob, rq, u, tx, txm, tg, tgm, tw, tp, si, so, pm, sh, uin, fwd, vin, inv,
-           w_sem, x1_send, x1_recv, x2_send, x2_recv, g1_send, g1_recv, gm_send, gm_recv, pair_sem,
-           sc_send, sc_recv, sd_sem, g2_send, g2_recv, up_send, up_recv, fw_sem):
+           wa, wc, sb, rb, ob, rq, u, tx, txm, tg, tgm, raw, rawm, tw, tp, tq, si, so, pm, uin, vin, at, nt, ya, inv,
+           w_sem, x1_send, x1_recv, x2_send, x2_recv, g1_send, g1_recv, gm_send, gm_recv, r1_send, r1_recv, rm_send, rm_recv, pair_sem,
+           sc_send, sc_recv, sd_sem, g2_send, g2_recv, up_send, up_recv):
     i = lax.axis_index("inst")
     a = lax.axis_index("axial")
     local, tiles, width = s0.shape
@@ -123,8 +123,9 @@
         sb[t, local:both, :] = f[:, t, :]
     row = lax.broadcasted_iota(jnp.int32, (cols, width), 0)
     col = lax.broadcasted_iota(jnp.int32, (cols, width), 1)
-    tx[0] = jnp.where(col == row + i * cols, 1.0, 0.0).astype(F32)
-    tx[1] = jnp.zeros((cols, width), F32)
+    tx[0, 0:cols] = jnp.where(col == row + i * cols, 1.0, 0.0).astype(F32)
+    tx[0, cols:] = jnp.zeros((both, width), F32)
+    tx[1] = jnp.zeros((cols + both, width), F32)
 
     pl.semaphore_wait(barrier, n_inst - 1 + jnp.where(
         hub, 2 + jnp.where(lead, NZ, 0) + jnp.where(y > 0, 1, 0), 0))
@@ -138,13 +139,19 @@
 
     def gather(src, dst, send, recv, xx, sender):
         half = pl.ds(pl.multiple_of(lax.rem(sender, 2) * cols, 8), cols)
-        return remote(src, dst.at[sender // 2, :, half], send.at[xx], recv.at[sender], inst=2 * xx + 1)
+        return remote(src.at[:, 0:cols], dst.at[sender // 2, :, half], send.at[xx], recv.at[sender], inst=2 * xx + 1)
 
     def whole(xx, sender):
         return gather(tx, tg, g1_send, g1_recv, xx, sender)
 
     def halfway(xx, sender):
         return gather(txm, tgm, gm_send, gm_recv, xx, sender)
+
+    def raw_whole(xx, sender):
+        return remote(tx.at[:, cols:cols + both], raw.at[sender], r1_send.at[xx], r1_recv.at[sender], inst=2 * xx + 1)
+
+    def raw_half(xx, sender):
+        return remote(txm.at[:, cols:cols + both], rawm.at[sender], rm_send.at[xx], rm_recv.at[sender], inst=2 * xx + 1)
 
     def to_hubs(copy):
         for xx in range(chips):
@@ -154,7 +161,6 @@
 
     other = i + 1 - 2 * core
     pass_rq = remote(rq, rq, pair_sem.at[0], pair_sem.at[1], inst=other)
-    share = remote(sh.at[0], sh.at[1], pair_sem.at[2], pair_sem.at[3], inst=other)
     give = remote(vin.at[0], vin.at[1], pair_sem.at[4], pair_sem.at[5], inst=other)
     early = remote(u.at[pl.ds(0, mid)], u.at[pl.ds(0, mid)], pair_sem.at[6], pair_sem.at[7], inst=other)
     late = remote(u.at[pl.ds(mid, mid)], u.at[pl.ds(mid, mid)], pair_sem.at[8], pair_sem.at[9], inst=other)
@@ -172,18 +178,51 @@
     load_a.wait()
     load_c.wait()
 
-    def column_step(k, carry):
+    def column_step(k):
         t = order[k]
         c, ai = wc[t], wa[t]
-        b = times(tx[...].reshape(block, width), c)
-        p = -times(b[:cols], ai)
+        b = times(tx[...].reshape(2 * (cols + both), width), c)
+        p = times(jnp.concatenate([-b[:cols], sb[t] - b[cols:cols + both]], 0), ai)
         tx[0] = p
-        tx[1] = -times(p + b[cols:], ai)
+        tx[1] = -times(p + b[cols + both:], ai)
+
+    def column_steps(first_tile, count):
+        def steps(n, carry):
+            for j in range(UNROLL):
+                column_step(first_tile + n * UNROLL + j)
+            return carry
+        lax.fori_loop(0, count // UNROLL, steps, 0)
+
+    column_steps(0, mid)
+    txm[...] = tx[...]
+    column_steps(mid, tiles - mid)
+    to_hubs(whole)
+    to_hubs(raw_whole)
+
+    pad = nt.shape[2] // 2
+
+    def prepare(n, carry):
+        t = order[mid * core + n]
+        turned = wa[t].T
+        at[n] = turned
+        high, low = halves(lax.dot_general(wc[t].T, turned, NN, preferred_element_type=F32))
+        nt[n, :, 0:width] = high
+        nt[n, :, pad:pad + width] = low
         return carry
 
-    lax.fori_loop(0, mid, column_step, 0)
-    txm[...] = tx[...]
-    lax.fori_loop(mid, MIX_AT, column_step, 0)
+    def drive(n, carry):
+        ya[n] = times(rq[order[mid * core + n]], at[n], NN)
+        return carry
+
+    def final_step(n, v):
+        m = lax.dot_general(split(v), nt[n], NN, preferred_element_type=F32)
+        m = m[:2 * both] + m[2 * both:]
+        r = ya[n] - (m[:, :width] + m[:, pad:pad + width])
+        g = r[both:] - times(r[:both], at[n], NN)
+        u[mid * core + n] = g
+        return jnp.concatenate([r[:both], g], 0)
+
+    zero = jnp.zeros((both, width), F32)
 
     @pl.when(core == 0)
     def _():
@@ -196,36 +235,16 @@
             mixed = jnp.dot(kmat[...], rb[:, t].reshape(both * n_inst, width),
                             precision=lax.Precision.HIGHEST, preferred_element_type=F32)
             ob[:, t] = mixed.reshape(chips, 2 * both, width)
+        lax.fori_loop(0, mid, prepare, 0)
         for d in range(1, chips):
             second(d).start()
         rq[pl.ds(per * x, per)] = ob[x]
-
-    lax.fori_loop(MIX_AT, tiles, column_step, 0)
-    to_hubs(whole)
-
-    def data_step(k, v):
-        t = order[k]
-        r = times(rq[t] - times(v, wc[t]), wa[t])
-        q = times(r[:both], wa[t])
-        return jnp.concatenate([r[:both], r[both:] - q], 0)
-
-    def final_step(k, v):
-        v = data_step(k, v)
-        u[k] = v[both:]
-        return v
-
-    zero = jnp.zeros((both, width), F32)
-
-    @pl.when(core == 0)
-    def _():
+        to_hubs(raw_half)
+        to_hubs(halfway)
         for d in range(1, chips):
             second(d).wait_recv()
         pass_rq.start()
-        v = lax.fori_loop(0, mid, data_step, jnp.zeros((2 * both, width), F32))
-        sh[0, 0] = v
-        sh[0, 1] = lax.fori_loop(mid, tiles, data_step, v)
-        share.start()
-        to_hubs(halfway)
+        lax.fori_loop(0, mid, drive, 0)
         give.wait_recv()
         lax.fori_loop(0, mid, final_step, vin[1])
         early.start()
@@ -233,7 +252,6 @@
         for t in range(tiles):
             out[:, t, :] = s0[:, t, :] + u[inv[t], 0:local, :]
         early.wait_send()
-        share.wait_send()
         pass_rq.wait_send()
         for d in range(1, chips):
             second(d).wait_send()
@@ -257,11 +275,17 @@
             return remote(uin.at[0], uin.at[1], up_send.at[zz], up_recv.at[0],
                           axial=lax.rem(y + 1, last + 1) * NZ + zz)
 
-        hop = remote(fwd.at[0], fwd.at[1], fw_sem.at[0], fw_sem.at[1], axial=y * NZ + lax.rem(z + 1, NZ))
+        def mix(rows):
+            made = [jnp.dot(kmat[pl.ds(pl.multiple_of(2 * both * x, 8), 2 * both)], rows[:, n].reshape(both * n_inst, width),
+                            precision=lax.Precision.HIGHEST, preferred_element_type=F32) for n in range(2)]
+            return made[0][:both], made[0][both:] + made[1][:both]
+
         count = jnp.where(y == 0, 0, chunks)
 
-        tg[x, :, pl.ds(cols, cols)] = tx[...]
-        tgm[x, :, pl.ds(cols, cols)] = txm[...]
+        tg[x, :, pl.ds(cols, cols)] = tx[:, 0:cols]
+        tgm[x, :, pl.ds(cols, cols)] = txm[:, 0:cols]
+        raw[i] = tx[:, cols:]
+        rawm[i] = txm[:, cols:]
         whole(0, i - 1).wait_recv()
 
         @pl.when((z == 0) & (y > 0))
@@ -269,6 +293,7 @@
             so[:, 0:block] = tg[x]
             lax.fori_loop(0, count, lambda c, k: (scan(c).start(), k)[1], 0)
 
+        lax.fori_loop(0, mid, prepare, 0)
         for j in range(n_inst):
             @pl.when((j != i) & (j != i - 1))
             def _(j=j):
@@ -280,6 +305,7 @@
                 for part in range(2):
                     store_map(tw, block * xx, part, tg[xx, part])
 
+        to_hubs(raw_half)
         to_hubs(halfway)
 
         @pl.when(z > 0)
@@ -288,31 +314,24 @@
                 scan(c).wait_recv()
                 part = pl.ds(pl.multiple_of(c * CHUNK, CHUNK), CHUNK)
 
-                @pl.when(jnp.logical_not(lead))
-                def _():
-                    for d in range(1, chips):
-                        spread(si, c, d).start()
-
-                @pl.when((y < last) | (z < NZ - 1))
+                @pl.when(z < NZ - 1)
                 def _():
                     p, g = through(tw, si[0, part], si[1, part])
                     so[0, part] = p
                     so[1, part] = g
-
-                @pl.when(z < NZ - 1)
-                def _():
                     scan(c).start()
 
-                @pl.when(lead)
-                def _():
-                    for d in range(1, chips):
-                        spread(so, c, d).start()
+                for d in range(1, chips):
+                    spread(si, c, d).start()
                 return carry
 
             lax.fori_loop(0, count, chunk_step, 0)
 
-        share.wait_recv()
-        bp, bg = sh[1, 1, 0:both], sh[1, 1, both:]
+        for j in range(n_inst):
+            @pl.when(j != i)
+            def _(j=j):
+                raw_whole(0, j).wait_recv()
+        bp, bg = mix(raw)
 
         @pl.when(z == 0)
         def _():
@@ -324,7 +343,7 @@
         def _():
             scan_data.wait_recv()
 
-            @pl.when((y < last) | (z < NZ - 1))
+            @pl.when((z < NZ - 1) | (y == 0))
             def _():
                 p, g = through(tw, si[0, data], si[1, data])
                 so[0, data] = p + bp
@@ -340,16 +359,36 @@
             for zz in range(NZ):
                 down(zz).start()
 
+        def give_out(p, g):
+            vin[0, 0:both] = p
+            vin[0, both:] = g
+            give.start()
+
+        @pl.when(y == 0)
+        def _():
+            @pl.when(z == 0)
+            def _():
+                give_out(zero, zero)
+
+            @pl.when(z > 0)
+            def _():
+                give_out(si[0, data], si[1, data])
+
+        pass_rq.wait_recv()
+        lax.fori_loop(0, mid, drive, 0)
+        for j in range(n_inst):
+            @pl.when(j != i)
+            def _(j=j):
+                raw_half(0, j).wait_recv()
+                halfway(0, j).wait_recv()
+        mp, mg = mix(rawm)
+        for xx in range(chips):
+            for part in range(2):
+                store_map(tq, block * xx, part, tgm[xx, part])
+
         @pl.when(mapped)
         def _():
-            @pl.when(lead)
-            def _():
-                pm[x] = so[:, 0:block]
-
-            @pl.when(jnp.logical_not(lead))
-            def _():
-                pm[x] = si[:, 0:block]
-
+            pm[x] = si[:, 0:block]
             for d in range(1, chips):
                 for c in range(chunks):
                     spread(si, c, d).wait_recv()
@@ -357,35 +396,6 @@
                 for part in range(2):
                     store_map(tp, block * xx, part, pm[xx, part])
 
-        def give_out(p, g):
-            vin[0, 0:both] = p
-            vin[0, both:] = g
-            give.start()
-
-        @pl.when(y == 0)
-        def _():
-            @pl.when(z == 0)
-            def _():
-                give_out(zero, zero)
-
-            @pl.when(z > 0)
-            def _():
-                give_out(si[0, data], si[1, data])
-
-        for j in range(n_inst):
-            @pl.when(j != i)
-            def _(j=j):
-                halfway(0, j).wait_recv()
-
-        def middle_map():
-            for xx in range(chips):
-                for part in range(2):
-                    store_map(tw, block * xx, part, tgm[xx, part])
-
-        @pl.when((y == 0) | (z != NZ - 2) | (y == last))
-        def _():
-            middle_map()
-
         @pl.when(y > 0)
         def _():
             down(0).wait_recv()
@@ -393,36 +403,24 @@
         @pl.when(mapped)
         def _():
             p, g = through(tp, uin[1, 0], uin[1, 1])
+            p, g = p + si[0, data], g + si[1, data]
 
             @pl.when(lead)
             def _():
-                uin[0, 0] = p + so[0, data]
-                uin[0, 1] = g + so[1, data]
+                next_p, next_g = through(tw, p, g)
+                uin[0, 0] = next_p + bp
+                uin[0, 1] = next_g + bg
                 for zz in range(NZ):
                     down(zz).start()
-                hop.wait_recv()
-                give_out(fwd[1, 0], fwd[1, 1])
-
-            @pl.when(jnp.logical_not(lead))
-            def _():
-                here_p, here_g = p + si[0, data], g + si[1, data]
-                give_out(here_p, here_g)
-
-                @pl.when((z == NZ - 2) & (y < last))
-                def _():
-                    next_p, next_g = through(tw, here_p, here_g)
-                    fwd[0, 0] = next_p + bp
-                    fwd[0, 1] = next_g + bg
-                    hop.start()
-                    middle_map()
+
+            give_out(p, g)
 
         @pl.when((y > 0) & (z == 0))
         def _():
             give_out(uin[1, 0], uin[1, 1])
 
-        p, g = through(tw, vin[0, 0:both], vin[0, both:])
-        pass_rq.wait_recv()
-        lax.fori_loop(mid, tiles, final_step, jnp.concatenate([p, g], 0) + sh[1, 0])
+        p, g = through(tq, vin[0, 0:both], vin[0, both:])
+        lax.fori_loop(0, mid, final_step, jnp.concatenate([p + mp, g + mg], 0))
         late.start()
         early.wait_recv()
         for t in range(tiles):
@@ -447,10 +445,6 @@
             for zz in range(NZ):
                 down(zz).wait_send()
 
-        @pl.when((y > 0) & (z == NZ - 2) & (y < last))
-        def _():
-            hop.wait_send()
-
     for xx in range(chips):
         @pl.when(2 * xx != i)
         def _(xx=xx):
@@ -460,6 +454,8 @@
         def _(xx=xx):
             whole(xx, i).wait_send()
             halfway(xx, i).wait_send()
+            raw_whole(xx, i).wait_send()
+            raw_half(xx, i).wait_send()
 
 
 def solution(mesh):
@@ -491,28 +487,32 @@
                 pltpu.VMEM((chips, per, 2 * both, width), F32),
                 pltpu.VMEM((tiles, 2 * both, width), F32),
                 pltpu.VMEM((tiles, both, width), F32),
-                pltpu.VMEM((2, cols, width), F32),
-                pltpu.VMEM((2, cols, width), F32),
+                pltpu.VMEM((2, cols + both, width), F32),
+                pltpu.VMEM((2, cols + both, width), F32),
                 pltpu.VMEM((chips, 2, block, width), F32),
                 pltpu.VMEM((chips, 2, block, width), F32),
+                pltpu.VMEM((n_inst, 2, both, width), F32),
+                pltpu.VMEM((n_inst, 2, both, width), F32),
+                pltpu.VMEM((width, 4 * pad), BF16),
                 pltpu.VMEM((width, 4 * pad), BF16),
                 pltpu.VMEM((width, 4 * pad), BF16),
                 pltpu.VMEM((2, block + both, width), F32),
                 pltpu.VMEM((2, block + both, width), F32),
                 pltpu.VMEM((chips, 2, block, width), F32),
-                pltpu.VMEM((2, 2, 2 * both, width), F32),
-                pltpu.VMEM((2, 2, both, width), F32),
                 pltpu.VMEM((2, 2, both, width), F32),
                 pltpu.VMEM((2, 2 * both, width), F32),
+                pltpu.VMEM((tiles // 2, width, width), BF16),
+                pltpu.VMEM((tiles // 2, width, 2 * pad), BF16),
+                pltpu.VMEM((tiles // 2, 2 * both, width), F32),
                 pltpu.SMEM((tiles,), jnp.int32),
                 dma((2,)),
                 dma((chips,)), dma((n_inst,)), dma((chips,)), dma((chips,)),
+                dma((chips,)), dma((n_inst,)), dma((chips,)), dma((n_inst,)),
                 dma((chips,)), dma((n_inst,)), dma((chips,)), dma((n_inst,)),
                 dma((10,)),
                 dma((chunks,)), dma((chunks,)), dma((2,)),
                 dma((chips - 1, chunks)), dma((chips - 1, chunks)),
                 dma((NZ,)), dma((1,)),
-                dma((2,)),
             ],
             compiler_params=pltpu.CompilerParams(collective_id=0, has_side_effects=True),
         )(sweep_order, kmat, flow_state, forcing, tile_inverse, coupling)

time: 63.4 us -> 62.7 us (0.989)
  no operation moved by 1% of the time
where the time goes in v4:
time: 62.7 us; the launch traced here: 61.9 us
  Pallas kernels  60.3 us (96%)
  local copies, waits for them, and re-layouts  1.54 us (2%)
    pallas_call x1, Pallas kernels, on_device(): pl.pallas_call(functools.partial(kernel, n_inst, n_axial), out_shape=jax....  60.3 us
    unnamed x1, local copies, waits for them, and re-layouts  1.54 us

profile of v4, /device:TPU:24, one launch (start us, length us, event | category | flops | bytes accessed | tf_op | source)
XLA Modules:
  0.0 61.9 jit_solution(1465949001598082546)
XLA Ops:
  0.0 60.3 %shard_map.64 = f32[4,16,320]{2,1,0:T(8,128)} custom-call(s32[16]{0:T(128)} %order.1, f32[64,64]{1,0:T(8,128)} %constant.2.clone.kmat, f32[4,16,320]{2,1,0:T(8,128)} %s0.1, f32[4,16,320]{2,1,0:T(8,128)} %f.1, bf16[16,320,320]{2,1,0:T(8,128)(2,1)} %a_hbm.1, bf16[16,320,320]{2,1,0:T(8,128)(2,1)} %c_hbm.1), custom_call_target="tpu_custom_call" | custom-call | tf_op jit(solution)/shard_map/pallas_call | solution.py:476
  60.3 1.5 %copy.8 = f32[4,16,320]{2,1,0:T(8,128)} copy(f32[4,16,320]{2,1,0:T(8,128)} %shard_map.64) | data formatting | bytes 163840

commit v5 on v4

--- a/solution.py
+++ b/solution.py
@@ -69,7 +69,7 @@
 
 
 def kernel(n_inst, n_axial, order, kmat, s0, f, a_hbm, c_hbm, out,
-           wa, wc, sb, rb, ob, rq, u, tx, txm, tg, tgm, raw, rawm, tw, tp, tq, si, so, pm, uin, vin, at, nt, ya, inv,
+           wa, wc, sb, rb, ob, rq, u, ps, gs, tx, txm, tg, tgm, raw, rawm, tw, tp, tq, si, so, pm, uin, vin, at, nt, ya, inv,
            w_sem, x1_send, x1_recv, x2_send, x2_recv, g1_send, g1_recv, gm_send, gm_recv, r1_send, r1_recv, rm_send, rm_recv, pair_sem,
            sc_send, sc_recv, sd_sem, g2_send, g2_recv, up_send, up_recv):
     i = lax.axis_index("inst")
@@ -123,12 +123,9 @@
         sb[t, local:both, :] = f[:, t, :]
     row = lax.broadcasted_iota(jnp.int32, (cols, width), 0)
     col = lax.broadcasted_iota(jnp.int32, (cols, width), 1)
-    tx[0, 0:cols] = jnp.where(col == row + i * cols, 1.0, 0.0).astype(F32)
-    tx[0, cols:] = jnp.zeros((both, width), F32)
-    tx[1] = jnp.zeros((cols + both, width), F32)
-
-    pl.semaphore_wait(barrier, n_inst - 1 + jnp.where(
-        hub, 2 + jnp.where(lead, NZ, 0) + jnp.where(y > 0, 1, 0), 0))
+    ps[0:cols] = jnp.where(col == row + i * cols, 1.0, 0.0).astype(F32)
+    ps[cols:] = jnp.zeros((both, width), F32)
+    gs[...] = jnp.zeros((cols + both, width), F32)
 
     def first(xx, sender):
         return remote(sb.at[pl.ds(per * xx, per)], rb.at[sender], x1_send.at[xx], x1_recv.at[sender], inst=2 * xx)
@@ -165,39 +162,60 @@
     early = remote(u.at[pl.ds(0, mid)], u.at[pl.ds(0, mid)], pair_sem.at[6], pair_sem.at[7], inst=other)
     late = remote(u.at[pl.ds(mid, mid)], u.at[pl.ds(mid, mid)], pair_sem.at[8], pair_sem.at[9], inst=other)
 
+    load_a.wait()
+    load_c.wait()
+
+    def nt_dot(v, w):
+        return lax.dot_general(v, w, NT, preferred_element_type=F32)
+
+    def joined(v):
+        m = v.shape[0] // 2
+        return v[:m] + v[m:]
+
+    def driven(t, b):
+        return jnp.concatenate([-b[:cols], sb[t] - b[cols:]], 0)
+
+    t = order[0]
+    ps[...] = times(driven(t, times(ps[...], wc[t])), wa[t])
+
+    def column_steps(start):
+        def steps(n, carry):
+            p, g = ps[...], gs[...]
+            for j in range(UNROLL):
+                k = start + n * UNROLL + j
+                before, here = order[k], order[jnp.minimum(k + 1, tiles - 1)]
+                high_p, high_g = split(p), split(g)
+                bp, bg = nt_dot(high_p, wc[here]), nt_dot(high_g, wc[before])
+                last_p = p
+                bp, bg = driven(here, joined(bp)), p + joined(bg)
+                p, g = nt_dot(split(bp), wa[here]), nt_dot(split(bg), wa[before])
+                p, g = joined(p), -joined(g)
+            ps[...] = p
+            gs[...] = g
+            tx[0] = last_p
+            return carry
+        lax.fori_loop(0, mid // UNROLL, steps, 0)
+        tx[1] = gs[...]
+
+    column_steps(0)
+    txm[...] = tx[...]
+
+    pl.semaphore_wait(barrier, n_inst - 1 + jnp.where(
+        hub, 2 + jnp.where(lead, NZ, 0) + jnp.where(y > 0, 1, 0), 0))
     for xx in range(chips):
         @pl.when(2 * xx != i)
         def _(xx=xx):
             first(xx, i).start()
+
+    column_steps(mid)
+    to_hubs(whole)
+    to_hubs(raw_whole)
+
     for t in range(tiles):
         pos = jnp.int32(0)
         for k in range(tiles):
             pos = jnp.where(order[k] == t, k, pos)
         inv[t] = pos
-
-    load_a.wait()
-    load_c.wait()
-
-    def column_step(k):
-        t = order[k]
-        c, ai = wc[t], wa[t]
-        b = times(tx[...].reshape(2 * (cols + both), width), c)
-        p = times(jnp.concatenate([-b[:cols], sb[t] - b[cols:cols + both]], 0), ai)
-        tx[0] = p
-        tx[1] = -times(p + b[cols + both:], ai)
-
-    def column_steps(first_tile, count):
-        def steps(n, carry):
-            for j in range(UNROLL):
-                column_step(first_tile + n * UNROLL + j)
-            return carry
-        lax.fori_loop(0, count // UNROLL, steps, 0)
-
-    column_steps(0, mid)
-    txm[...] = tx[...]
-    column_steps(mid, tiles - mid)
-    to_hubs(whole)
-    to_hubs(raw_whole)
 
     pad = nt.shape[2] // 2
 
@@ -214,13 +232,18 @@
         ya[n] = times(rq[order[mid * core + n]], at[n], NN)
         return carry
 
-    def final_step(n, v):
-        m = lax.dot_general(split(v), nt[n], NN, preferred_element_type=F32)
-        m = m[:2 * both] + m[2 * both:]
-        r = ya[n] - (m[:, :width] + m[:, pad:pad + width])
-        g = r[both:] - times(r[:both], at[n], NN)
-        u[mid * core + n] = g
-        return jnp.concatenate([r[:both], g], 0)
+    def by_pair(v, n):
+        m = joined(lax.dot_general(split(v), nt[n], NN, preferred_element_type=F32))
+        return m[:, :width] + m[:, pad:pad + width]
+
+    def rerun(p, g):
+        p = ya[0, 0:both] - by_pair(p, 0)
+        for n in range(mid):
+            old = p
+            if n + 1 < mid:
+                p = ya[n + 1, 0:both] - by_pair(old, n + 1)
+            g = ya[n, both:] - by_pair(g, n) - times(old, at[n], NN)
+            u[mid * core + n] = g
 
     zero = jnp.zeros((both, width), F32)
 
@@ -246,7 +269,7 @@
         pass_rq.start()
         lax.fori_loop(0, mid, drive, 0)
         give.wait_recv()
-        lax.fori_loop(0, mid, final_step, vin[1])
+        rerun(vin[1, 0:both], vin[1, both:])
         early.start()
         late.wait_recv()
         for t in range(tiles):
@@ -420,7 +443,7 @@
             give_out(uin[1, 0], uin[1, 1])
 
         p, g = through(tq, vin[0, 0:both], vin[0, both:])
-        lax.fori_loop(0, mid, final_step, jnp.concatenate([p + mp, g + mg], 0))
+        rerun(p + mp, g + mg)
         late.start()
         early.wait_recv()
         for t in range(tiles):
@@ -487,6 +510,8 @@
                 pltpu.VMEM((chips, per, 2 * both, width), F32),
                 pltpu.VMEM((tiles, 2 * both, width), F32),
                 pltpu.VMEM((tiles, both, width), F32),
+                pltpu.VMEM((cols + both, width), F32),
+                pltpu.VMEM((cols + both, width), F32),
                 pltpu.VMEM((2, cols + both, width), F32),
                 pltpu.VMEM((2, cols + both, width), F32),
                 pltpu.VMEM((chips, 2, block, width), F32),

time: 62.7 us -> 58.3 us (0.930)
  Pallas kernels: 60.3 us -> 55.8 us
    pallas_call x1, Pallas kernels: 60.3 us -> 55.8 us  [on_device(): pl.pallas_call(functools.partial(kernel, n_inst, n_axial), out_shape=jax....]
where the time goes in v5:
time: 58.3 us; the launch traced here: 57.4 us
  Pallas kernels  55.8 us (96%)
  local copies, waits for them, and re-layouts  1.54 us (3%)
    pallas_call x1, Pallas kernels, on_device(): pl.pallas_call(functools.partial(kernel, n_inst, n_axial), out_shape=jax....  55.8 us
    unnamed x1, local copies, waits for them, and re-layouts  1.54 us

profile of v5, /device:TPU:24, one launch (start us, length us, event | category | flops | bytes accessed | tf_op | source)
XLA Modules:
  0.0 57.4 jit_solution(18092029215014405907)
XLA Ops:
  0.0 55.8 %shard_map.64 = f32[4,16,320]{2,1,0:T(8,128)} custom-call(s32[16]{0:T(128)} %order.1, f32[64,64]{1,0:T(8,128)} %constant.2.clone.kmat, f32[4,16,320]{2,1,0:T(8,128)} %s0.1, f32[4,16,320]{2,1,0:T(8,128)} %f.1, bf16[16,320,320]{2,1,0:T(8,128)(2,1)} %a_hbm.1, bf16[16,320,320]{2,1,0:T(8,128)(2,1)} %c_hbm.1), custom_call_target="tpu_custom_call" | custom-call | tf_op jit(solution)/shard_map/pallas_call | solution.py:499
  55.9 1.5 %copy.8 = f32[4,16,320]{2,1,0:T(8,128)} copy(f32[4,16,320]{2,1,0:T(8,128)} %shard_map.64) | data formatting | bytes 163840

commit v6 on v5

--- a/solution.py
+++ b/solution.py
@@ -11,6 +11,7 @@
 ITERS = 2
 SPECTRAL_GAIN = 2.0
 NZ = 8
+VMEM_BYTES = 56_400_000
 UNROLL = 4
 CHUNK = 16
 MESH = pl.DeviceIdType.MESH
@@ -68,8 +69,8 @@
     return y[:rows, :width], y[rows:, :width] + y[:rows, pad:pad + width]
 
 
-def kernel(n_inst, n_axial, order, kmat, s0, f, a_hbm, c_hbm, out,
-           wa, wc, sb, rb, ob, rq, u, ps, gs, tx, txm, tg, tgm, raw, rawm, tw, tp, tq, si, so, pm, uin, vin, at, nt, ya, inv,
+def kernel(n_inst, n_axial, order, k_hbm, s_hbm, f_hbm, a_hbm, c_hbm, out,
+           kmat, s0, f, wa, wc, sb, rb, ob, rq, u, ps, gs, tx, txm, tg, tgm, raw, rawm, tw, tp, tq, si, so, pm, uin, vin, at, nt, ya, inv,
            w_sem, x1_send, x1_recv, x2_send, x2_recv, g1_send, g1_recv, gm_send, gm_recv, r1_send, r1_recv, rm_send, rm_recv, pair_sem,
            sc_send, sc_recv, sd_sem, g2_send, g2_recv, up_send, up_recv):
     i = lax.axis_index("inst")
@@ -90,10 +91,10 @@
     mapped = (y > 0) & (z > 0)
     data = pl.ds(block, both)
 
-    load_a = pltpu.make_async_copy(a_hbm, wa, w_sem.at[0])
-    load_c = pltpu.make_async_copy(c_hbm, wc, w_sem.at[1])
-    load_a.start()
-    load_c.start()
+    loads = [pltpu.make_async_copy(src, dst, w_sem.at[n]) for n, (src, dst) in enumerate(
+        [(s_hbm, s0), (f_hbm, f), (c_hbm, wc), (a_hbm, wa), (k_hbm.at[pl.ds(0, kmat.shape[0])], kmat)])]
+    for load in loads:
+        load.start()
 
     def remote(src, dst, send, recv, **there):
         return pltpu.make_async_remote_copy(
@@ -118,6 +119,8 @@
         def _():
             pl.semaphore_signal(barrier, inc=1, device_id={"axial": y * NZ - 1}, device_id_type=MESH)
 
+    loads[0].wait()
+    loads[1].wait()
     for t in range(tiles):
         sb[t, 0:local, :] = s0[:, t, :]
         sb[t, local:both, :] = f[:, t, :]
@@ -162,8 +165,8 @@
     early = remote(u.at[pl.ds(0, mid)], u.at[pl.ds(0, mid)], pair_sem.at[6], pair_sem.at[7], inst=other)
     late = remote(u.at[pl.ds(mid, mid)], u.at[pl.ds(mid, mid)], pair_sem.at[8], pair_sem.at[9], inst=other)
 
-    load_a.wait()
-    load_c.wait()
+    for load in loads[2:]:
+        load.wait()
 
     def nt_dot(v, w):
         return lax.dot_general(v, w, NT, preferred_element_type=F32)
@@ -255,7 +258,7 @@
             def _(j=j):
                 first(0, j).wait_recv()
         for t in range(per):
-            mixed = jnp.dot(kmat[...], rb[:, t].reshape(both * n_inst, width),
+            mixed = jnp.dot(kmat[:, 0:both * n_inst], rb[:, t].reshape(both * n_inst, width),
                             precision=lax.Precision.HIGHEST, preferred_element_type=F32)
             ob[:, t] = mixed.reshape(chips, 2 * both, width)
         lax.fori_loop(0, mid, prepare, 0)
@@ -299,7 +302,7 @@
                           axial=lax.rem(y + 1, last + 1) * NZ + zz)
 
         def mix(rows):
-            made = [jnp.dot(kmat[pl.ds(pl.multiple_of(2 * both * x, 8), 2 * both)], rows[:, n].reshape(both * n_inst, width),
+            made = [jnp.dot(kmat[pl.ds(pl.multiple_of(2 * both * x, 8), 2 * both), 0:both * n_inst], rows[:, n].reshape(both * n_inst, width),
                             precision=lax.Precision.HIGHEST, preferred_element_type=F32) for n in range(2)]
             return made[0][:both], made[0][both:] + made[1][:both]
 
@@ -493,16 +496,22 @@
         pad = -(-width // 128) * 128
         both = 2 * local
         chunks = block // CHUNK
-        kmat = jnp.asarray(exchange_matrix(local * n_inst, n_inst))
+        size = both * n_inst
+        kmat = np.zeros((10 * size, 128), np.float32)
+        kmat[:size, :size] = exchange_matrix(local * n_inst, n_inst)
+        kmat = jnp.asarray(kmat)
+        hbm = pl.BlockSpec(memory_space=pl.ANY)
         vmem = pl.BlockSpec(memory_space=pltpu.VMEM)
         dma = pltpu.SemaphoreType.DMA
         return pl.pallas_call(
             functools.partial(kernel, n_inst, n_axial),
             out_shape=jax.ShapeDtypeStruct(flow_state.shape, F32),
-            in_specs=[pl.BlockSpec(memory_space=pltpu.SMEM), vmem, vmem, vmem,
-                      pl.BlockSpec(memory_space=pl.ANY), pl.BlockSpec(memory_space=pl.ANY)],
+            in_specs=[pl.BlockSpec(memory_space=pltpu.SMEM), hbm, hbm, hbm, hbm, hbm],
             out_specs=vmem,
             scratch_shapes=[
+                pltpu.VMEM((size, 128), F32),
+                pltpu.VMEM(flow_state.shape, F32),
+                pltpu.VMEM(flow_state.shape, F32),
                 pltpu.VMEM((tiles, width, width), BF16),
                 pltpu.VMEM((tiles, width, width), BF16),
                 pltpu.VMEM((tiles, both, width), F32),
@@ -530,7 +539,7 @@
                 pltpu.VMEM((tiles // 2, width, 2 * pad), BF16),
                 pltpu.VMEM((tiles // 2, 2 * both, width), F32),
                 pltpu.SMEM((tiles,), jnp.int32),
-                dma((2,)),
+                dma((5,)),
                 dma((chips,)), dma((n_inst,)), dma((chips,)), dma((chips,)),
                 dma((chips,)), dma((n_inst,)), dma((chips,)), dma((n_inst,)),
                 dma((chips,)), dma((n_inst,)), dma((chips,)), dma((n_inst,)),
@@ -539,7 +548,7 @@
                 dma((chips - 1, chunks)), dma((chips - 1, chunks)),
                 dma((NZ,)), dma((1,)),
             ],
-            compiler_params=pltpu.CompilerParams(collective_id=0, has_side_effects=True),
+            compiler_params=pltpu.CompilerParams(collective_id=0, has_side_effects=True, vmem_limit_bytes=VMEM_BYTES),
         )(sweep_order, kmat, flow_state, forcing, tile_inverse, coupling)
 
     return jax.shard_map(

time: 58.3 us -> 57.1 us (0.979)
  Pallas kernels: 55.8 us -> 54.9 us
    pallas_call x1, Pallas kernels: 55.8 us -> 54.9 us  [on_device(): pl.pallas_call(functools.partial(kernel, n_inst, n_axial), out_shape=jax....]
    unnamed x1 -> x3, local copies, waits for them, and re-layouts: 1.54 us -> 1.3 us
where the time goes in v6:
time: 57.1 us; the launch traced here: 56.2 us
  Pallas kernels  54.9 us (96%)
  local copies, waits for them, and re-layouts  1.3 us (2%)
    pallas_call x1, Pallas kernels, on_device(): pl.pallas_call(functools.partial(kernel, n_inst, n_axial), out_shape=jax....  54.9 us
    unnamed x3, local copies, waits for them, and re-layouts  1.3 us

profile of v6, /device:TPU:24, one launch (start us, length us, event | category | flops | bytes accessed | tf_op | source)
XLA Modules:
  0.0 56.2 jit_solution(4305179285626498461)
XLA Ops:
  0.0 0.0 copy-start
  0.0 0.7 %copy-done = s32[16]{0:T(128)S(1)} copy-done((s32[16]{0:T(128)S(1)}, s32[16]{0:T(128)}, u32[]{:S(2)}) %copy-start) | copy-done | bytes 88
  0.7 54.9 %shard_map.64 = f32[4,16,320]{2,1,0:T(8,128)S(1)} custom-call(s32[16]{0:T(128)S(1)} %copy-done, f32[640,128]{1,0:T(8,128)} %constant.2.clone.k_hbm, f32[4,16,320]{2,1,0:T(8,128)} %s_hbm.1, f32[4,16,320]{2,1,0:T(8,128)} %f_hbm.1, bf16[16,320,320]{2,1,0:T(8,128)(2,1)} %a_hbm.1, bf16[16,320,320]{2,1,0:T(8,128)(2,1)} %c_hbm.1), custom_call_target="tpu_custom_call" | custom-call | tf_op jit(solution)/shard_map/pallas_call | solution.py:506
  55.6 0.6 %copy.8 = f32[4,16,320]{2,1,0:T(8,128)} copy(f32[4,16,320]{2,1,0:T(8,128)S(1)} %shard_map.64) | data formatting | bytes 163840
Async XLA Ops:
  0.0 0.7 %copy-start = (s32[16]{0:T(128)S(1)}, s32[16]{0:T(128)}, u32[]{:S(2)}) copy-start(s32[16]{0:T(128)} %order.1) | copy-start | bytes 196

commit v7 on v6

--- a/solution.py
+++ b/solution.py
@@ -12,6 +12,7 @@
 SPECTRAL_GAIN = 2.0
 NZ = 8
 VMEM_BYTES = 56_400_000
+FAR_FIRST, FAR_LAST = (2, 1, 3), (1, 3, 2)
 UNROLL = 4
 CHUNK = 16
 MESH = pl.DeviceIdType.MESH
@@ -52,12 +53,27 @@
     return y[:m] + y[m:]
 
 
-def store_map(dst, row, part, block):
+def pack(p, g):
+    whole = p.shape[1] // 128 * 128
+    return jnp.concatenate([p[:, :whole], g[:, :whole], p[:, whole:], g[:, whole:]], 1)
+
+
+def unpack(b):
+    width = b.shape[1] // 2
+    whole = width // 128 * 128
+    middle = whole + width
+    return (jnp.concatenate([b[:, :whole], b[:, 2 * whole:middle]], 1),
+            jnp.concatenate([b[:, whole:2 * whole], b[:, middle:]], 1))
+
+
+def store_map(dst, row, block):
     pad = dst.shape[1] // 4
-    rows, width = block.shape
-    high, low = halves(block)
-    dst[pl.ds(row, rows), part * pad:part * pad + width] = high
-    dst[pl.ds(row, rows), (2 + part) * pad:(2 + part) * pad + width] = low
+    for part, rows in enumerate(unpack(block)):
+        width = rows.shape[1]
+        at = pl.ds(pl.multiple_of(row, 16), rows.shape[0])
+        high, low = halves(rows)
+        dst[at, part * pad:part * pad + width] = high
+        dst[at, (2 + part) * pad:(2 + part) * pad + width] = low
 
 
 def through(m, p, g):
@@ -70,7 +86,7 @@
 
 
 def kernel(n_inst, n_axial, order, k_hbm, s_hbm, f_hbm, a_hbm, c_hbm, out,
-           kmat, s0, f, wa, wc, sb, rb, ob, rq, u, ps, gs, tx, txm, tg, tgm, raw, rawm, tw, tp, tq, si, so, pm, uin, vin, at, nt, ya, inv,
+           kmat, s0, f, wa, wc, sb, rb, ob, rq, u, ps, gs, pv, tx, txm, tg, tgm, raw, rawm, tw, tp, tq, si, so, pm, uin, vin, at, nt, ya, inv,
            w_sem, x1_send, x1_recv, x2_send, x2_recv, g1_send, g1_recv, gm_send, gm_recv, r1_send, r1_recv, rm_send, rm_recv, pair_sem,
            sc_send, sc_recv, sd_sem, g2_send, g2_recv, up_send, up_recv):
     i = lax.axis_index("inst")
@@ -139,7 +155,7 @@
 
     def gather(src, dst, send, recv, xx, sender):
         half = pl.ds(pl.multiple_of(lax.rem(sender, 2) * cols, 8), cols)
-        return remote(src.at[:, 0:cols], dst.at[sender // 2, :, half], send.at[xx], recv.at[sender], inst=2 * xx + 1)
+        return remote(src.at[0:cols], dst.at[sender // 2, half], send.at[xx], recv.at[sender], inst=2 * xx + 1)
 
     def whole(xx, sender):
         return gather(tx, tg, g1_send, g1_recv, xx, sender)
@@ -148,10 +164,10 @@
         return gather(txm, tgm, gm_send, gm_recv, xx, sender)
 
     def raw_whole(xx, sender):
-        return remote(tx.at[:, cols:cols + both], raw.at[sender], r1_send.at[xx], r1_recv.at[sender], inst=2 * xx + 1)
+        return remote(tx.at[cols:cols + both], raw.at[sender], r1_send.at[xx], r1_recv.at[sender], inst=2 * xx + 1)
 
     def raw_half(xx, sender):
-        return remote(txm.at[:, cols:cols + both], rawm.at[sender], rm_send.at[xx], rm_recv.at[sender], inst=2 * xx + 1)
+        return remote(txm.at[cols:cols + both], rawm.at[sender], rm_send.at[xx], rm_recv.at[sender], inst=2 * xx + 1)
 
     def to_hubs(copy):
         for xx in range(chips):
@@ -181,7 +197,7 @@
     t = order[0]
     ps[...] = times(driven(t, times(ps[...], wc[t])), wa[t])
 
-    def column_steps(start):
+    def column_steps(start, made):
         def steps(n, carry):
             p, g = ps[...], gs[...]
             for j in range(UNROLL):
@@ -195,13 +211,12 @@
                 p, g = joined(p), -joined(g)
             ps[...] = p
             gs[...] = g
-            tx[0] = last_p
+            pv[...] = last_p
             return carry
         lax.fori_loop(0, mid // UNROLL, steps, 0)
-        tx[1] = gs[...]
-
-    column_steps(0)
-    txm[...] = tx[...]
+        made[...] = pack(pv[...], gs[...])
+
+    column_steps(0, txm)
 
     pl.semaphore_wait(barrier, n_inst - 1 + jnp.where(
         hub, 2 + jnp.where(lead, NZ, 0) + jnp.where(y > 0, 1, 0), 0))
@@ -210,7 +225,7 @@
         def _(xx=xx):
             first(xx, i).start()
 
-    column_steps(mid)
+    column_steps(mid, tx)
     to_hubs(whole)
     to_hubs(raw_whole)
 
@@ -286,15 +301,15 @@
     def _():
         def scan(c):
             part = pl.ds(pl.multiple_of(c * CHUNK, CHUNK), CHUNK)
-            return remote(so.at[:, part], si.at[:, part], sc_send.at[c], sc_recv.at[c],
+            return remote(so.at[part], si.at[part], sc_send.at[c], sc_recv.at[c],
                           axial=y * NZ + lax.rem(z + 1, NZ))
 
-        scan_data = remote(so.at[:, data], si.at[:, data], sd_sem.at[0], sd_sem.at[1],
+        scan_data = remote(so.at[data], si.at[data], sd_sem.at[0], sd_sem.at[1],
                            axial=y * NZ + lax.rem(z + 1, NZ))
 
         def spread(src, c, d):
             part = pl.ds(pl.multiple_of(c * CHUNK, CHUNK), CHUNK)
-            return remote(src.at[:, part], pm.at[x, :, part], g2_send.at[d - 1, c], g2_recv.at[d - 1, c],
+            return remote(src.at[part], pm.at[x, part], g2_send.at[d - 1, c], g2_recv.at[d - 1, c],
                           inst=lax.rem(i + 2 * d, n_inst))
 
         def down(zz):
@@ -302,34 +317,31 @@
                           axial=lax.rem(y + 1, last + 1) * NZ + zz)
 
         def mix(rows):
-            made = [jnp.dot(kmat[pl.ds(pl.multiple_of(2 * both * x, 8), 2 * both), 0:both * n_inst], rows[:, n].reshape(both * n_inst, width),
-                            precision=lax.Precision.HIGHEST, preferred_element_type=F32) for n in range(2)]
+            made = [jnp.dot(kmat[pl.ds(pl.multiple_of(2 * both * x, 8), 2 * both), 0:both * n_inst], part,
+                            precision=lax.Precision.HIGHEST, preferred_element_type=F32)
+                    for part in unpack(rows[...].reshape(both * n_inst, 2 * width))]
             return made[0][:both], made[0][both:] + made[1][:both]
 
         count = jnp.where(y == 0, 0, chunks)
 
-        tg[x, :, pl.ds(cols, cols)] = tx[:, 0:cols]
-        tgm[x, :, pl.ds(cols, cols)] = txm[:, 0:cols]
-        raw[i] = tx[:, cols:]
-        rawm[i] = txm[:, cols:]
+        tg[x, pl.ds(cols, cols)] = tx[0:cols]
+        tgm[x, pl.ds(cols, cols)] = txm[0:cols]
+        raw[i] = tx[cols:]
+        rawm[i] = txm[cols:]
         whole(0, i - 1).wait_recv()
 
         @pl.when((z == 0) & (y > 0))
         def _():
-            so[:, 0:block] = tg[x]
+            so[0:block] = tg[x]
             lax.fori_loop(0, count, lambda c, k: (scan(c).start(), k)[1], 0)
 
         lax.fori_loop(0, mid, prepare, 0)
-        for j in range(n_inst):
-            @pl.when((j != i) & (j != i - 1))
-            def _(j=j):
-                whole(0, j).wait_recv()
-
-        @pl.when(z > 0)
-        def _():
-            for xx in range(chips):
-                for part in range(2):
-                    store_map(tw, block * xx, part, tg[xx, part])
+        store_map(tw, block * x, tg[x])
+        for d in FAR_LAST:
+            there = lax.rem(x + d, chips)
+            for j in range(2):
+                whole(0, 2 * there + j).wait_recv()
+            store_map(tw, block * there, tg[there])
 
         to_hubs(raw_half)
         to_hubs(halfway)
@@ -342,12 +354,10 @@
 
                 @pl.when(z < NZ - 1)
                 def _():
-                    p, g = through(tw, si[0, part], si[1, part])
-                    so[0, part] = p
-                    so[1, part] = g
+                    so[part] = pack(*through(tw, *unpack(si[part])))
                     scan(c).start()
 
-                for d in range(1, chips):
+                for d in FAR_FIRST:
                     spread(si, c, d).start()
                 return carry
 
@@ -361,8 +371,7 @@
 
         @pl.when(z == 0)
         def _():
-            so[0, data] = bp
-            so[1, data] = bg
+            so[data] = pack(bp, bg)
             scan_data.start()
 
         @pl.when(z > 0)
@@ -371,9 +380,8 @@
 
             @pl.when((z < NZ - 1) | (y == 0))
             def _():
-                p, g = through(tw, si[0, data], si[1, data])
-                so[0, data] = p + bp
-                so[1, data] = g + bg
+                p, g = through(tw, *unpack(si[data]))
+                so[data] = pack(p + bp, g + bg)
 
             @pl.when(z < NZ - 1)
             def _():
@@ -381,7 +389,7 @@
 
         @pl.when((y == 0) & (z == NZ - 1))
         def _():
-            uin[0] = so[:, data]
+            uin[0] = so[data]
             for zz in range(NZ):
                 down(zz).start()
 
@@ -398,7 +406,7 @@
 
             @pl.when(z > 0)
             def _():
-                give_out(si[0, data], si[1, data])
+                give_out(*unpack(si[data]))
 
         pass_rq.wait_recv()
         lax.fori_loop(0, mid, drive, 0)
@@ -409,18 +417,16 @@
                 halfway(0, j).wait_recv()
         mp, mg = mix(rawm)
         for xx in range(chips):
-            for part in range(2):
-                store_map(tq, block * xx, part, tgm[xx, part])
+            store_map(tq, block * xx, tgm[xx])
 
         @pl.when(mapped)
         def _():
-            pm[x] = si[:, 0:block]
-            for d in range(1, chips):
+            store_map(tp, block * x, si[0:block])
+            for d in FAR_LAST:
+                there = lax.rem(x + chips - d, chips)
                 for c in range(chunks):
                     spread(si, c, d).wait_recv()
-            for xx in range(chips):
-                for part in range(2):
-                    store_map(tp, block * xx, part, pm[xx, part])
+                store_map(tp, block * there, pm[there])
 
         @pl.when(y > 0)
         def _():
@@ -428,14 +434,14 @@
 
         @pl.when(mapped)
         def _():
-            p, g = through(tp, uin[1, 0], uin[1, 1])
-            p, g = p + si[0, data], g + si[1, data]
+            p, g = through(tp, *unpack(uin[1]))
+            own_p, own_g = unpack(si[data])
+            p, g = p + own_p, g + own_g
 
             @pl.when(lead)
             def _():
                 next_p, next_g = through(tw, p, g)
-                uin[0, 0] = next_p + bp
-                uin[0, 1] = next_g + bg
+                uin[0] = pack(next_p + bp, next_g + bg)
                 for zz in range(NZ):
                     down(zz).start()
 
@@ -443,7 +449,7 @@
 
         @pl.when((y > 0) & (z == 0))
         def _():
-            give_out(uin[1, 0], uin[1, 1])
+            give_out(*unpack(uin[1]))
 
         p, g = through(tq, vin[0, 0:both], vin[0, both:])
         rerun(p + mp, g + mg)
@@ -521,19 +527,20 @@
                 pltpu.VMEM((tiles, both, width), F32),
                 pltpu.VMEM((cols + both, width), F32),
                 pltpu.VMEM((cols + both, width), F32),
-                pltpu.VMEM((2, cols + both, width), F32),
-                pltpu.VMEM((2, cols + both, width), F32),
-                pltpu.VMEM((chips, 2, block, width), F32),
-                pltpu.VMEM((chips, 2, block, width), F32),
-                pltpu.VMEM((n_inst, 2, both, width), F32),
-                pltpu.VMEM((n_inst, 2, both, width), F32),
+                pltpu.VMEM((cols + both, width), F32),
+                pltpu.VMEM((cols + both, 2 * width), F32),
+                pltpu.VMEM((cols + both, 2 * width), F32),
+                pltpu.VMEM((chips, block, 2 * width), F32),
+                pltpu.VMEM((chips, block, 2 * width), F32),
+                pltpu.VMEM((n_inst, both, 2 * width), F32),
+                pltpu.VMEM((n_inst, both, 2 * width), F32),
                 pltpu.VMEM((width, 4 * pad), BF16),
                 pltpu.VMEM((width, 4 * pad), BF16),
                 pltpu.VMEM((width, 4 * pad), BF16),
-                pltpu.VMEM((2, block + both, width), F32),
-                pltpu.VMEM((2, block + both, width), F32),
-                pltpu.VMEM((chips, 2, block, width), F32),
-                pltpu.VMEM((2, 2, both, width), F32),
+                pltpu.VMEM((block + both, 2 * width), F32),
+                pltpu.VMEM((block + both, 2 * width), F32),
+                pltpu.VMEM((chips, block, 2 * width), F32),
+                pltpu.VMEM((2, both, 2 * width), F32),
                 pltpu.VMEM((2, 2 * both, width), F32),
                 pltpu.VMEM((tiles // 2, width, width), BF16),
                 pltpu.VMEM((tiles // 2, width, 2 * pad), BF16),

time: 57.1 us -> 55.1 us (0.965)
  Pallas kernels: 54.9 us -> 53.1 us
    pallas_call x1, Pallas kernels: 54.9 us -> 53.1 us  [on_device(): pl.pallas_call(functools.partial(kernel, n_inst, n_axial), out_shape=jax....]
where the time goes in v7:
time: 55.1 us; the launch traced here: 54.4 us
  Pallas kernels  53.1 us (96%)
  local copies, waits for them, and re-layouts  1.3 us (2%)
    pallas_call x1, Pallas kernels, on_device(): pl.pallas_call(functools.partial(kernel, n_inst, n_axial), out_shape=jax....  53.1 us
    unnamed x3, local copies, waits for them, and re-layouts  1.3 us

profile of v7, /device:TPU:24, one launch (start us, length us, event | category | flops | bytes accessed | tf_op | source)
XLA Modules:
  0.0 54.4 jit_solution(625466330616803731)
XLA Ops:
  0.0 0.0 copy-start
  0.0 0.7 %copy-done = s32[16]{0:T(128)S(1)} copy-done((s32[16]{0:T(128)S(1)}, s32[16]{0:T(128)}, u32[]{:S(2)}) %copy-start) | copy-done | bytes 88
  0.7 53.1 %shard_map.64 = f32[4,16,320]{2,1,0:T(8,128)S(1)} custom-call(s32[16]{0:T(128)S(1)} %copy-done, f32[640,128]{1,0:T(8,128)} %constant.2.clone.k_hbm, f32[4,16,320]{2,1,0:T(8,128)} %s_hbm.1, f32[4,16,320]{2,1,0:T(8,128)} %f_hbm.1, bf16[16,320,320]{2,1,0:T(8,128)(2,1)} %a_hbm.1, bf16[16,320,320]{2,1,0:T(8,128)(2,1)} %c_hbm.1), custom_call_target="tpu_custom_call" | custom-call | tf_op jit(solution)/shard_map/pallas_call | solution.py:512
  53.8 0.6 %copy.8 = f32[4,16,320]{2,1,0:T(8,128)} copy(f32[4,16,320]{2,1,0:T(8,128)S(1)} %shard_map.64) | data formatting | bytes 163840
Async XLA Ops:
  0.0 0.7 %copy-start = (s32[16]{0:T(128)S(1)}, s32[16]{0:T(128)}, u32[]{:S(2)}) copy-start(s32[16]{0:T(128)} %order.1) | copy-start | bytes 196

commit v8 on v7

--- a/solution.py
+++ b/solution.py
@@ -14,7 +14,7 @@
 VMEM_BYTES = 56_400_000
 FAR_FIRST, FAR_LAST = (2, 1, 3), (1, 3, 2)
 UNROLL = 4
-CHUNK = 16
+CHUNK = 8
 MESH = pl.DeviceIdType.MESH
 F32, BF16 = jnp.float32, jnp.bfloat16
 NT = (((1,), (1,)), ((), ()))

time: 55.1 us -> 54.2 us (0.984)
  Pallas kernels: 53.1 us -> 52.1 us
    pallas_call x1, Pallas kernels: 53.1 us -> 52.1 us  [on_device(): pl.pallas_call(functools.partial(kernel, n_inst, n_axial), out_shape=jax....]
where the time goes in v8:
time: 54.2 us; the launch traced here: 53.4 us
  Pallas kernels  52.1 us (96%)
  local copies, waits for them, and re-layouts  1.3 us (2%)
    pallas_call x1, Pallas kernels, on_device(): pl.pallas_call(functools.partial(kernel, n_inst, n_axial), out_shape=jax....  52.1 us
    unnamed x3, local copies, waits for them, and re-layouts  1.3 us

profile of v8, /device:TPU:24, one launch (start us, length us, event | category | flops | bytes accessed | tf_op | source)
XLA Modules:
  0.0 53.4 jit_solution(9491674534659710167)
XLA Ops:
  0.0 0.0 copy-start
  0.0 0.7 %copy-done = s32[16]{0:T(128)S(1)} copy-done((s32[16]{0:T(128)S(1)}, s32[16]{0:T(128)}, u32[]{:S(2)}) %copy-start) | copy-done | bytes 88
  0.7 52.1 %shard_map.64 = f32[4,16,320]{2,1,0:T(8,128)S(1)} custom-call(s32[16]{0:T(128)S(1)} %copy-done, f32[640,128]{1,0:T(8,128)} %constant.2.clone.k_hbm, f32[4,16,320]{2,1,0:T(8,128)} %s_hbm.1, f32[4,16,320]{2,1,0:T(8,128)} %f_hbm.1, bf16[16,320,320]{2,1,0:T(8,128)(2,1)} %a_hbm.1, bf16[16,320,320]{2,1,0:T(8,128)(2,1)} %c_hbm.1), custom_call_target="tpu_custom_call" | custom-call | tf_op jit(solution)/shard_map/pallas_call | solution.py:512
  52.8 0.6 %copy.8 = f32[4,16,320]{2,1,0:T(8,128)} copy(f32[4,16,320]{2,1,0:T(8,128)S(1)} %shard_map.64) | data formatting | bytes 163840
Async XLA Ops:
  0.0 0.7 %copy-start = (s32[16]{0:T(128)S(1)}, s32[16]{0:T(128)}, u32[]{:S(2)}) copy-start(s32[16]{0:T(128)} %order.1) | copy-start | bytes 196

commit v9 on v8

--- a/solution.py
+++ b/solution.py
@@ -79,9 +79,10 @@
 def through(m, p, g):
     rows, width = p.shape
     pad = m.shape[1] // 4
-    y = lax.dot_general(split(jnp.concatenate([p, g], 0)), m[...], NN, preferred_element_type=F32)
-    y = y[:2 * rows] + y[2 * rows:]
-    y = y[:, :2 * pad] + y[:, 2 * pad:]
+    x = jnp.concatenate([p, g], 0)
+    y = lax.dot_general(split(x), m[:, 0:2 * pad], NN, preferred_element_type=F32)
+    z = lax.dot_general(x.astype(BF16), m[:, 2 * pad:], NN, preferred_element_type=F32)
+    y = y[:2 * rows] + y[2 * rows:] + z
     return y[:rows, :width], y[rows:, :width] + y[:rows, pad:pad + width]
 
 

time: 54.2 us -> 54 us (level)
  no operation moved by 1% of the time
where the time goes in v9:
time: 54 us; the launch traced here: 53.2 us
  Pallas kernels  51.9 us (96%)
  local copies, waits for them, and re-layouts  1.3 us (2%)
    pallas_call x1, Pallas kernels, on_device(): pl.pallas_call(functools.partial(kernel, n_inst, n_axial), out_shape=jax....  51.9 us
    unnamed x3, local copies, waits for them, and re-layouts  1.3 us

profile of v9, /device:TPU:24, one launch (start us, length us, event | category | flops | bytes accessed | tf_op | source)
XLA Modules:
  0.0 53.2 jit_solution(3565002941188845257)
XLA Ops:
  0.0 0.0 copy-start
  0.0 0.7 %copy-done = s32[16]{0:T(128)S(1)} copy-done((s32[16]{0:T(128)S(1)}, s32[16]{0:T(128)}, u32[]{:S(2)}) %copy-start) | copy-done | bytes 88
  0.7 51.9 %shard_map.64 = f32[4,16,320]{2,1,0:T(8,128)S(1)} custom-call(s32[16]{0:T(128)S(1)} %copy-done, f32[640,128]{1,0:T(8,128)} %constant.2.clone.k_hbm, f32[4,16,320]{2,1,0:T(8,128)} %s_hbm.1, f32[4,16,320]{2,1,0:T(8,128)} %f_hbm.1, bf16[16,320,320]{2,1,0:T(8,128)(2,1)} %a_hbm.1, bf16[16,320,320]{2,1,0:T(8,128)(2,1)} %c_hbm.1), custom_call_target="tpu_custom_call" | custom-call | tf_op jit(solution)/shard_map/pallas_call | solution.py:513
  52.6 0.6 %copy.8 = f32[4,16,320]{2,1,0:T(8,128)} copy(f32[4,16,320]{2,1,0:T(8,128)S(1)} %shard_map.64) | data formatting | bytes 163840
Async XLA Ops:
  0.0 0.7 %copy-start = (s32[16]{0:T(128)S(1)}, s32[16]{0:T(128)}, u32[]{:S(2)}) copy-start(s32[16]{0:T(128)} %order.1) | copy-start | bytes 196

commit v10 on v9

--- a/solution.py
+++ b/solution.py
@@ -13,7 +13,7 @@
 NZ = 8
 VMEM_BYTES = 56_400_000
 FAR_FIRST, FAR_LAST = (2, 1, 3), (1, 3, 2)
-UNROLL = 4
+UNROLL = 8
 CHUNK = 8
 MESH = pl.DeviceIdType.MESH
 F32, BF16 = jnp.float32, jnp.bfloat16

time: 54 us -> 53.6 us (level)
  no operation moved by 1% of the time
where the time goes in v10:
time: 53.6 us; the launch traced here: 52.9 us
  Pallas kernels  51.6 us (96%)
  local copies, waits for them, and re-layouts  1.3 us (2%)
    pallas_call x1, Pallas kernels, on_device(): pl.pallas_call(functools.partial(kernel, n_inst, n_axial), out_shape=jax....  51.6 us
    unnamed x3, local copies, waits for them, and re-layouts  1.3 us

profile of v10, /device:TPU:24, one launch (start us, length us, event | category | flops | bytes accessed | tf_op | source)
XLA Modules:
  0.0 52.9 jit_solution(4320605939004997629)
XLA Ops:
  0.0 0.0 copy-start
  0.0 0.7 %copy-done = s32[16]{0:T(128)S(1)} copy-done((s32[16]{0:T(128)S(1)}, s32[16]{0:T(128)}, u32[]{:S(2)}) %copy-start) | copy-done | bytes 88
  0.7 51.6 %shard_map.64 = f32[4,16,320]{2,1,0:T(8,128)S(1)} custom-call(s32[16]{0:T(128)S(1)} %copy-done, f32[640,128]{1,0:T(8,128)} %constant.2.clone.k_hbm, f32[4,16,320]{2,1,0:T(8,128)} %s_hbm.1, f32[4,16,320]{2,1,0:T(8,128)} %f_hbm.1, bf16[16,320,320]{2,1,0:T(8,128)(2,1)} %a_hbm.1, bf16[16,320,320]{2,1,0:T(8,128)(2,1)} %c_hbm.1), custom_call_target="tpu_custom_call" | custom-call | tf_op jit(solution)/shard_map/pallas_call | solution.py:513
  52.2 0.6 %copy.8 = f32[4,16,320]{2,1,0:T(8,128)} copy(f32[4,16,320]{2,1,0:T(8,128)S(1)} %shard_map.64) | data formatting | bytes 163840
Async XLA Ops:
  0.0 0.7 %copy-start = (s32[16]{0:T(128)S(1)}, s32[16]{0:T(128)}, u32[]{:S(2)}) copy-start(s32[16]{0:T(128)} %order.1) | copy-start | bytes 196
